TPU v7x, 32 devices: a whole 2x2x4 slice. The times are simulated.
32 devices in a mesh: groups: 2 (over x), node: 8 (over z, y), rep: 2 (over core).
Axes of the slice: x: 2, y: 2, z: 4, core: 2. Of those that a mesh axis runs over, the one named last changes fastest.
Arguments:
- normed_input: bfloat16 [4, 1024, 5120], P(('groups', 'rep'), 'node'), parts along dimension 0, may hold values from -6 to 6
- queries: bfloat16 [4, 1024, 2560], P(('groups', 'rep'), 'node'), parts along dimension 0, may hold values from -120 to 120
- rotated_key_heads: bfloat16 [4, 1024, 512], P(('groups', 'rep'), 'node'), parts along dimension 0, may hold values from -6 to 6
- frozen_value_rows: bfloat16 [4, 1024, 512], P(('groups', 'rep'), 'node'), parts along dimension 0, may hold values from -6 to 6
- adapter_down_weight: bfloat16 [5120, 32], replicated, may hold values from -0.078125 to 0.078125
- adapter_up_weight: bfloat16 [32, 512], replicated, may hold values from -1 to 1
- output_gradient: bfloat16 [4, 1024, 2560], P(('groups', 'rep'), 'node'), parts along dimension 0, may hold values from -6 to 6
- parents: int32 [4, 8], P(('groups', 'rep')), parts along dimension 0, may hold values from -1 to 6, as said below
- lengths: int32 [4, 8], P(('groups', 'rep')), parts along dimension 0, may hold values from 32 to 128, as said below
Outputs:
- attended: bfloat16 [4, 1024, 2560], P(('groups', 'rep'), 'node'), parts along dimension 0
- query_grad: bfloat16 [4, 1024, 2560], P(('groups', 'rep'), 'node'), parts along dimension 0
- down_grad: float32 [10240, 32], P('groups'), parts along dimension 0
- up_grad: float32 [64, 512], P('groups'), parts along dimension 0
There are 2 independent parts, one for each index of `groups`. A program takes and returns all parts, laid end to end along the dimension named above; an argument that names none is the same for every part. Nothing has to cross between parts.
Inputs may be any that keep to these rules, and one draw needn't show every extreme that they name: `parents`: slots 0 to 1 form the shared prompt, each the parent of the next, slot 0 the root. Every other slot's parent is slot 1 or a slot below it, and every ancestor of a slot s outside the prompt lies among the slots s - 5 to s - 1. `lengths`: prompt blocks are full.
All inputs are finite; a program needn't handle non-finite values.
Results may differ from a plain program's by a relative error of at most 0.0062.
Values may be sent and summed in bfloat16 or wider, within the bound.
A program may use at most 128 MiB of HBM per device.

v0:
```python
import functools
import math

import jax
import jax.numpy as jnp
from jax import lax
from jax.experimental import pallas as pl
from jax.experimental.pallas import tpu as pltpu
from jax.sharding import PartitionSpec as P

KEY_HEADS = 4
HEAD_SIZE = 128
PROMPT = 2
SPAN = 5
STEPS = 1 + PROMPT + SPAN
NEGATIVE = -1e30
F32 = jnp.float32
BF16 = jnp.bfloat16
NT = (((1,), (1,)), ((), ()))
NN = (((1,), (0,)), ((), ()))
TN = (((0,), (0,)), ((), ()))


def dot(a, b, dims):
    return lax.dot_general(a, b, dims, preferred_element_type=F32)


def attention_kernel(
    parents, lengths, q_ref, g_ref, own_k, own_v, own_low, k_ref, v_ref, low_ref, up_ref,
    att_ref, qg_ref, proj_ref, upg_ref,
    cand, score, out_acc, qg_acc, grad,
):
    own = lax.axis_index("node")
    head = pl.program_id(0)
    slots, block, _ = k_ref.shape
    per = q_ref.shape[1] // HEAD_SIZE
    rows = per * block
    scale = HEAD_SIZE ** -0.5

    cand[0] = own
    current = own
    count = jnp.int32(1)
    for step in range(1, STEPS):
        parent = parents[0, jnp.maximum(current, 0)]
        current = jnp.where(current >= 0, parent, -1)
        cand[step] = jnp.maximum(current, 0)
        count = count + (current >= 0).astype(jnp.int32)
    own_length = lengths[0, own]

    def stack(ref):
        return jnp.concatenate(
            [ref[:, c * HEAD_SIZE:(c + 1) * HEAD_SIZE] for c in range(per)], axis=0
        )

    live = lax.broadcasted_iota(jnp.int32, (block, HEAD_SIZE), 0) < own_length
    for c in range(per):
        part = g_ref[:, c * HEAD_SIZE:(c + 1) * HEAD_SIZE].astype(F32)
        grad[pl.ds(c * block, block), :] = jnp.where(live, part, 0.0).astype(BF16)
    query = stack(q_ref)

    column = lax.broadcasted_iota(jnp.int32, (block, block), 1)
    row = lax.broadcasted_iota(jnp.int32, (block, block), 0)

    s = dot(query, own_k[...], NT) * (scale * math.log2(math.e))
    allowed = (column <= row) & (column < own_length)
    bias = jnp.where(allowed, 0.0, NEGATIVE)
    bias = jnp.concatenate([bias] * per, axis=0)
    s = jnp.where(bias < 0.0, NEGATIVE, s)
    score[0] = s

    def logits_step(h, top):
        slot = cand[h]
        s = dot(query, k_ref[slot], NT) * (scale * math.log2(math.e))
        col = lax.broadcasted_iota(jnp.int32, (rows, block), 1)
        s = jnp.where(col < lengths[0, slot], s, NEGATIVE)
        score[h] = s
        return jnp.maximum(top, s)

    top = lax.fori_loop(1, count, logits_step, s)
    top = jnp.max(top, axis=1, keepdims=True)

    def exp_step(h, total):
        e = jnp.exp2(score[h] - top)
        score[h] = e
        return total + e

    total = lax.fori_loop(0, count, exp_step, jnp.zeros((rows, block), F32))
    inverse = 1.0 / jnp.sum(total, axis=1, keepdims=True)

    w = score[0] * inverse
    score[0] = w
    out_acc[...] = dot(w.astype(BF16), own_v[...], NN)

    def output_step(h, carry):
        w = score[h] * inverse
        score[h] = w
        out_acc[...] += dot(w.astype(BF16), v_ref[cand[h]], NN)
        return carry

    lax.fori_loop(1, count, output_step, 0)

    dots = jnp.sum(grad[...].astype(F32) * out_acc[...], axis=1, keepdims=True)
    for c in range(per):
        part = out_acc[pl.ds(c * block, block), :]
        att_ref[:, c * HEAD_SIZE:(c + 1) * HEAD_SIZE] = jnp.where(live, part, 0.0).astype(BF16)

    @pl.when(head == 0)
    def _():
        proj_ref[...] = jnp.zeros_like(proj_ref)

    def backward(h, slot, key, value, low):
        g = grad[...]
        w = score[h]
        pressure = dot(g, value, NT)
        slopes = (w * (pressure - dots) * scale).astype(BF16)
        query_part = dot(slopes, key, NN)
        value_grad = dot(w.astype(BF16), g, TN)
        high = value_grad.astype(BF16)
        lowp = (value_grad - high.astype(F32)).astype(BF16)
        proj_ref[slot] += dot(up_ref[...], high, NT) + dot(up_ref[...], lowp, NT)
        return query_part, dot(low, high, NN) + dot(low, lowp, NN)

    qg_acc[...], upg_ref[...] = backward(0, own, own_k[...], own_v[...], own_low[...])

    def backward_step(h, carry):
        slot = cand[h]
        query_part, up_part = backward(h, slot, k_ref[slot], v_ref[slot], low_ref[slot])
        qg_acc[...] += query_part
        upg_ref[...] += up_part
        return carry

    lax.fori_loop(1, count, backward_step, 0)
    for c in range(per):
        qg_ref[:, c * HEAD_SIZE:(c + 1) * HEAD_SIZE] = qg_acc[pl.ds(c * block, block), :].astype(BF16)


def attention(parents, lengths, q, g, k, v, low, k_all, v_all, low_all, up):
    slots, block, width = k_all.shape
    heads = width // HEAD_SIZE
    rank = up.shape[0]
    group = q.shape[1] // heads
    rows = group // HEAD_SIZE * block
    smem = pl.BlockSpec(memory_space=pltpu.SMEM)
    return pl.pallas_call(
        attention_kernel,
        grid=(heads,),
        in_specs=[
            smem, smem,
            pl.BlockSpec((block, group), lambda k: (0, k)),
            pl.BlockSpec((block, group), lambda k: (0, k)),
            pl.BlockSpec((block, HEAD_SIZE), lambda k: (0, k)),
            pl.BlockSpec((block, HEAD_SIZE), lambda k: (0, k)),
            pl.BlockSpec((rank, block), lambda k: (0, 0)),
            pl.BlockSpec((slots, block, HEAD_SIZE), lambda k: (0, 0, k)),
            pl.BlockSpec((slots, block, HEAD_SIZE), lambda k: (0, 0, k)),
            pl.BlockSpec((slots, rank, block), lambda k: (0, 0, 0)),
            pl.BlockSpec((rank, HEAD_SIZE), lambda k: (0, k)),
        ],
        out_specs=[
            pl.BlockSpec((block, group), lambda k: (0, k)),
            pl.BlockSpec((block, group), lambda k: (0, k)),
            pl.BlockSpec((slots, rank, block), lambda k: (0, 0, 0)),
            pl.BlockSpec((rank, HEAD_SIZE), lambda k: (0, k)),
        ],
        out_shape=[
            jax.ShapeDtypeStruct(q.shape, BF16),
            jax.ShapeDtypeStruct(q.shape, BF16),
            jax.ShapeDtypeStruct((slots, rank, block), F32),
            jax.ShapeDtypeStruct((rank, width), F32),
        ],
        scratch_shapes=[
            pltpu.SMEM((STEPS,), jnp.int32),
            pltpu.VMEM((STEPS, rows, block), F32),
            pltpu.VMEM((rows, HEAD_SIZE), F32),
            pltpu.VMEM((rows, HEAD_SIZE), F32),
            pltpu.VMEM((rows, HEAD_SIZE), BF16),
        ],
        compiler_params=pltpu.CompilerParams(
            dimension_semantics=("arbitrary",), vmem_limit_bytes=48 * 1024 * 1024
        ),
        name="tree_attention",
    )(parents, lengths, q, g, k, v, low, k_all, v_all, low_all, up)


def peer(node, rep=None):
    target = {"node": node}
    if rep is not None:
        target["rep"] = rep
    return target


def greet(slots, reps):
    own, rep = lax.axis_index("node"), lax.axis_index("rep")
    barrier = pltpu.get_barrier_semaphore()
    for step in range(reps):
        other = lax.rem(rep + step, lax.axis_size("rep"))

        def signal(t, carry):
            pl.semaphore_signal(
                barrier, inc=1, device_id=peer(lax.rem(own + t, slots), other),
                device_id_type=pl.DeviceIdType.MESH,
            )
            return carry

        lax.fori_loop(0 if step else 1, slots, signal, 0)
    pl.semaphore_wait(barrier, slots * reps - 1)


def reaches(slot, below):
    return (below > slot) & ((slot < PROMPT) | (below - slot <= SPAN))


def share_kernel(slots, *refs):
    own = lax.axis_index("node")
    sources, targets, (send_sem, recv_sem) = refs[:3], refs[3:6], refs[6:]
    pair = own // 2
    partner = own + 1 - 2 * lax.rem(own, 2)
    greet(slots, 1)

    def copies(refs, slot, way, target):
        return [
            pltpu.make_async_remote_copy(
                src_ref=refs[i] if refs is sources else refs[i].at[slot],
                dst_ref=targets[i].at[slot],
                send_sem=send_sem.at[way, i, slot], recv_sem=recv_sem.at[i, slot],
                device_id=peer(target), device_id_type=pl.DeviceIdType.MESH,
            )
            for i in range(3)
        ]

    def onward(slot):
        return (own + 2 < slots) & reaches(slot, 2 * pair + 2)

    def each_way(refs, slot, action):
        @pl.when(onward(slot))
        def _():
            for c in copies(refs, slot, 0, own + 2):
                action(c)

        @pl.when(reaches(slot, partner))
        def _():
            for c in copies(refs, slot, 1, partner):
                action(c)

    def relayed(action):
        def body(step, carry):
            slot = own - 2 * step

            @pl.when(reaches(slot, 2 * pair))
            def _():
                action(slot)
            return carry

        lax.fori_loop(1, pair + 1, body, 0)

    def arrived(slot):
        for c in copies(targets, slot, 1, partner):
            c.wait_recv()

    def forward(slot):
        arrived(slot)
        each_way(targets, slot, lambda c: c.start())

    each_way(sources, own, lambda c: c.start())
    relayed(forward)

    def from_partner(step, carry):
        slot = partner - 2 * step

        @pl.when(reaches(slot, own))
        def _():
            arrived(slot)
        return carry

    lax.fori_loop(0, pair + 1, from_partner, 0)
    each_way(sources, own, lambda c: c.wait_send())
    relayed(lambda slot: each_way(targets, slot, lambda c: c.wait_send()))


def share(slots, *arrays):
    anywhere = pl.BlockSpec(memory_space=pl.ANY)
    return pl.pallas_call(
        functools.partial(share_kernel, slots),
        in_specs=[anywhere] * 3,
        out_specs=[anywhere] * 3,
        out_shape=[jax.ShapeDtypeStruct((slots, *a.shape), a.dtype) for a in arrays],
        scratch_shapes=[
            pltpu.SemaphoreType.DMA((2, 3, slots)),
            pltpu.SemaphoreType.DMA((3, slots)),
        ],
        compiler_params=pltpu.CompilerParams(collective_id=0, has_side_effects=True),
        name="share_blocks",
    )(*arrays)


def combine_kernel(
    slots, reps, factor, proj, x_ref, upg_ref, down_ref, up_ref,
    landed, total, parts, gathered, result,
    send_p, recv_p, send_r, recv_r, send_g, recv_g,
):
    own, rep = lax.axis_index("node"), lax.axis_index("rep")
    width = x_ref.shape[1]
    up_width = upg_ref.shape[1]
    _, chunks, half, chunk = parts.shape
    mesh_id = pl.DeviceIdType.MESH
    greet(slots, reps)

    def scatter(source, target):
        return pltpu.make_async_remote_copy(
            src_ref=proj.at[target], dst_ref=landed.at[source],
            send_sem=send_p.at[target], recv_sem=recv_p.at[source],
            device_id=peer(target), device_id_type=mesh_id,
        )

    def scatter_start(t, carry):
        @pl.when(reaches(t, own))
        def _():
            scatter(own, t).start()
        return carry

    lax.fori_loop(0, slots, scatter_start, 0)
    total[...] = proj[own]

    def scatter_add(t, carry):
        @pl.when(reaches(own, t))
        def _():
            pltpu.make_async_remote_copy(
                src_ref=proj.at[t], dst_ref=landed.at[t],
                send_sem=send_p.at[t], recv_sem=recv_p.at[t],
                device_id=peer(t), device_id_type=mesh_id,
            ).wait_recv()
            total[...] += landed[t]
        return carry

    lax.fori_loop(0, slots, scatter_add, 0)
    projected = total[...].astype(BF16)
    rank = projected.shape[0]
    for j in range(chunks):
        low, high = j * chunk, (j + 1) * chunk
        pieces = []
        if low < width:
            pieces.append(dot(projected, x_ref[:, low:min(high, width)], NN))
        if high > width and low < width + up_width:
            pieces.append(upg_ref[:, max(low - width, 0):min(high - width, up_width)])
        filled = sum(p.shape[1] for p in pieces)
        if filled < chunk:
            pieces.append(jnp.zeros((rank, chunk - filled), F32))
        value = (pieces[0] if len(pieces) == 1 else jnp.concatenate(pieces, axis=1)).astype(BF16)
        for r in range(reps):
            parts[r, j] = value[r * half:(r + 1) * half]

    def reduce_copy(source, node, r, from_rep):
        return pltpu.make_async_remote_copy(
            src_ref=parts.at[r, node], dst_ref=gathered.at[from_rep, source],
            send_sem=send_r.at[r, node], recv_sem=recv_r.at[from_rep, source],
            device_id=peer(node, r), device_id_type=mesh_id,
        )

    def gather_copy(node, r, owner, owner_rep):
        return pltpu.make_async_remote_copy(
            src_ref=result.at[owner_rep, owner], dst_ref=result.at[owner_rep, owner],
            send_sem=send_g.at[r, node], recv_sem=recv_g.at[owner_rep, owner],
            device_id=peer(node, r), device_id_type=mesh_id,
        )

    def others(action):
        for step in range(reps):
            r = lax.rem(rep + step, reps)

            def body(t, carry):
                action(lax.rem(own + t, slots), r)
                return carry

            lax.fori_loop(0 if step else 1, slots, body, 0)

    def reduce_start(node, r):
        @pl.when(node < chunks)
        def _():
            reduce_copy(own, node, r, rep).start()

    others(reduce_start)

    @pl.when(own < chunks)
    def _():
        gathered[rep, own] = parts[rep, own]

        def reduce_wait(node, r):
            reduce_copy(node, own, rep, r).wait_recv()

        others(reduce_wait)

        def add(t, acc):
            for r in range(reps):
                acc = acc + gathered[r, t].astype(F32)
            return acc

        acc = lax.fori_loop(0, slots, add, jnp.zeros((half, chunk), F32))
        result[rep, own] = (acc * factor).astype(BF16)

        def gather_start(node, r):
            gather_copy(node, r, own, rep).start()

        others(gather_start)

    def gather_wait(node, r):
        @pl.when(node < chunks)
        def _():
            gather_copy(own, rep, node, r).wait_recv()

    others(gather_wait)
    for j in range(chunks):
        low, high = j * chunk, (j + 1) * chunk
        for r in range(reps):
            rows = slice(r * half, (r + 1) * half)
            if low < width:
                end = min(high, width)
                down_ref[rows, low:end] = result[r, j, :, :end - low].astype(F32)
            if high > width and low < width + up_width:
                a, b = max(low, width), min(high, width + up_width)
                up_ref[rows, a - width:b - width] = result[r, j, :, a - low:b - low].astype(F32)

    def scatter_drain(t, carry):
        @pl.when(reaches(t, own))
        def _():
            scatter(own, t).wait_send()
        return carry

    lax.fori_loop(0, slots, scatter_drain, 0)

    def reduce_drain(node, r):
        @pl.when(node < chunks)
        def _():
            reduce_copy(own, node, r, rep).wait_send()

    others(reduce_drain)

    @pl.when(own < chunks)
    def _():
        others(lambda node, r: gather_copy(node, r, own, rep).wait_send())


def combine(slots, reps, factor, proj, x, upg):
    _, rank, block = proj.shape
    width, up_width = x.shape[1], upg.shape[1]
    tiles = -(-(width + up_width) // 128)
    per = -(-tiles // slots)
    chunks = -(-tiles // per)
    chunk = per * 128
    half = rank // reps
    vmem = pl.BlockSpec(memory_space=pltpu.VMEM)
    dma = pltpu.SemaphoreType.DMA
    return pl.pallas_call(
        functools.partial(combine_kernel, slots, reps, factor),
        in_specs=[vmem] * 3,
        out_specs=[vmem] * 2,
        out_shape=[
            jax.ShapeDtypeStruct((rank, width), F32),
            jax.ShapeDtypeStruct((rank, up_width), F32),
        ],
        scratch_shapes=[
            pltpu.VMEM(proj.shape, F32),
            pltpu.VMEM((rank, block), F32),
            pltpu.VMEM((reps, chunks, half, chunk), BF16),
            pltpu.VMEM((reps, slots, half, chunk), BF16),
            pltpu.VMEM((reps, chunks, half, chunk), BF16),
            dma((slots,)), dma((slots,)),
            dma((reps, slots)), dma((reps, slots)),
            dma((reps, slots)), dma((reps, slots)),
        ],
        compiler_params=pltpu.CompilerParams(
            collective_id=1, has_side_effects=True, vmem_limit_bytes=48 * 1024 * 1024
        ),
        name="combine_gradients",
    )(proj, x, upg)


def on_device(x, q, k, frozen, down, up, g, parents, lengths):
    x, q, k, frozen, g = x[0], q[0], k[0], frozen[0], g[0]
    block = x.shape[0]
    slots = lax.axis_size("node")
    low_t = lax.dot_general(
        down, x, (((0,), (1,)), ((), ())), preferred_element_type=F32
    ).astype(BF16)
    values = (frozen.astype(F32) + dot(low_t, up, TN)).astype(BF16)
    k_all, v_all, low_all = share(slots, k, values, low_t)
    attended, query_grad, proj, up_sum = attention(
        parents, lengths, q, g, k, values, low_t, k_all, v_all, low_all, up
    )
    reps = lax.axis_size("rep")
    factor = (slots * reps * block) ** -0.5
    down_sum, up_total = combine(slots, reps, factor, proj, x, up_sum)
    return attended[None], query_grad[None], down_sum.T, up_total


def solution(mesh):
    rows = P(("groups", "rep"), "node", None)
    table = P(("groups", "rep"), None)
    return jax.shard_map(
        on_device,
        mesh=mesh,
        in_specs=(rows, rows, rows, rows, P(), P(), rows, table, table),
        out_specs=(rows, rows, P("groups", None), P("groups", None)),
        check_vma=False,
    )
```

profile of v0, /device:TPU:0, one launch (start us, length us, event | category | flops | bytes accessed | tf_op | source)
XLA Modules:
  0.0 102.9 jit_solution(4131298601303493748)
XLA Ops:
  0.6 0.0 copy-start
  0.6 0.0 copy-start.8
  0.7 0.0 copy-start.13
  0.7 0.0 copy-start.12
  0.7 0.0 copy-start.6
  0.7 0.0 copy-start.14
  0.7 0.0 copy-start.7
  0.7 0.0 copy-start.5
  0.7 0.9 copy-done
  1.6 1.8 %convolution_convert_fusion.refs_2_.own_low = bf16[32,128]{1,0:T(8,128)(2,1)S(1)} fusion(bf16[5120,32]{0,1:T(8,128)(2,1)S(1)} %copy-done, bf16[1,128,5120]{2,1,0:T(8,128)(2,1)} %param.9), kind=kOutput, calls=%fused_computation.2 | convolution fusion | flops 41947136 | bytes 1646592 | tf_op jit(solution)/shard_map/dot_general | solution.py:481
  3.5 0.0 copy-done.8
  3.5 0.0 copy-done.14
  3.5 0.0 copy-start.9
  3.5 0.9 fusion.refs_1_.own_v
  4.4 0.0 copy-done.9
  4.4 12.7 %share_blocks.1 = (bf16[8,128,512]{2,1,0:T(8,128)(2,1)}, bf16[8,128,512]{2,1,0:T(8,128)(2,1)}, bf16[8,32,128]{2,1,0:T(8,128)(2,1)}) custom-call(bf16[128,512]{1,0:T(8,128)(2,1)} %bitcast.19, bf16[128,512]{1,0:T(8,128)(2,1)} %fusion.refs_1_.own_v, bf16[32,128]{1,0:T(8,128)(2,1)} %copy-done.9), custom_call_target="tpu_custom_call" | custom-call | tf_op jit(solution)/shard_map/share_blocks/pallas_call | solution.py:282
  17.1 0.0 copy-done.13
  17.1 0.0 copy-done.12
  17.1 0.0 copy-done.6
  17.1 0.0 copy-done.7
  17.1 0.0 copy-done.5
  17.1 0.0 copy-start.2
  17.1 0.9 copy-done.2
  18.0 0.0 copy-start.3
  18.0 1.2 %copy-done.3 = bf16[8,128,512]{2,1,0:T(8,128)(2,1)S(1)} copy-done((bf16[8,128,512]{2,1,0:T(8,128)(2,1)S(1)}, bf16[8,128,512]{2,1,0:T(8,128)(2,1)}, u32[]{:S(2)}) %copy-start.3) | copy-done | bytes 1048600
  19.2 0.0 copy-start.4
  19.2 1.2 %copy-done.4 = bf16[8,128,512]{2,1,0:T(8,128)(2,1)S(1)} copy-done((bf16[8,128,512]{2,1,0:T(8,128)(2,1)S(1)}, bf16[8,128,512]{2,1,0:T(8,128)(2,1)}, u32[]{:S(2)}) %copy-start.4) | copy-done | bytes 1048600
  20.5 0.0 copy-start.10
  20.5 0.7 copy-done.10
  21.2 0.0 copy-start.11
  21.2 0.8 copy-done.11
  22.0 0.0 copy-start.1
  22.0 7.9 %tree_attention.1 = (bf16[128,2560]{1,0:T(8,128)(2,1)}, bf16[128,2560]{1,0:T(8,128)(2,1)}, f32[8,32,128]{2,1,0:T(8,128)S(1)}, f32[32,512]{1,0:T(8,128)S(1)}) custom-call(s32[1,8]{1,0:T(1,128)S(1)} %copy-done.12, s32[1,8]{1,0:T(1,128)S(1)} %copy-done.13, bf16[128,2560]{1,0:T(8,128)(2,1)S(1)} %bitcast.17, bf16[128,2560]{1,0:T(8,128)(2,1)S(1)} %bitcast.18, ...), custom_call_target="tpu_custom_call" | custom-call | tf_op jit(solution)/shard_map/tree_attention/pallas_call | solution.py:144
  29.9 0.0 copy-done.1
  29.9 71.5 %combine_gradients.1 = (f32[32,5120]{1,0:T(8,128)S(1)}, f32[32,512]{1,0:T(8,128)S(1)}) custom-call(f32[8,32,128]{2,1,0:T(8,128)S(1)} %get-tuple-element.18.proj, bf16[128,5120]{1,0:T(8,128)(2,1)S(1)} %bitcast.15, f32[32,512]{1,0:T(8,128)S(1)} %get-tuple-element.19.upg_ref), custom_call_target="tpu_custom_call" | custom-call | tf_op jit(solution)/shard_map/combine_gradients/pallas_call | solution.py:452
  101.4 0.8 copy.15
  102.3 0.6 copy.16
Async XLA Ops:
  0.6 1.0 copy-start
  0.6 2.8 %copy-start.8 = (bf16[32,512]{1,0:T(8,128)(2,1)S(1)}, bf16[32,512]{1,0:T(8,128)(2,1)}, u32[]{:S(2)}) copy-start(bf16[32,512]{1,0:T(8,128)(2,1)} %up_ref.1) | copy-start | bytes 98308
  0.7 16.4 %copy-start.13 = (s32[1,8]{1,0:T(1,128)S(1)}, s32[1,8]{1,0:T(1,128)}, u32[]{:S(2)}) copy-start(s32[1,8]{1,0:T(1,128)} %lengths.1) | copy-start | bytes 100
  0.7 16.4 %copy-start.12 = (s32[1,8]{1,0:T(1,128)S(1)}, s32[1,8]{1,0:T(1,128)}, u32[]{:S(2)}) copy-start(s32[1,8]{1,0:T(1,128)} %parents.1) | copy-start | bytes 100
  0.7 16.4 %copy-start.6 = (bf16[1,128,2560]{2,1,0:T(8,128)(2,1)S(1)}, bf16[1,128,2560]{2,1,0:T(8,128)(2,1)}, u32[]{:S(2)}) copy-start(bf16[1,128,2560]{2,1,0:T(8,128)(2,1)} %param.15) | copy-start | bytes 1966084
  0.7 2.8 %copy-start.14 = (bf16[1,128,512]{2,1,0:T(8,128)(2,1)S(1)}, bf16[1,128,512]{2,1,0:T(8,128)(2,1)}, u32[]{:S(2)}) copy-start(bf16[1,128,512]{2,1,0:T(8,128)(2,1)} %param.12) | copy-start | bytes 393220
  0.7 16.4 %copy-start.7 = (bf16[1,128,512]{2,1,0:T(8,128)(2,1)S(1)}, bf16[1,128,512]{2,1,0:T(8,128)(2,1)}, u32[]{:S(2)}) copy-start(bf16[1,128,512]{2,1,0:T(8,128)(2,1)} %param.11) | copy-start | bytes 393220
  0.7 16.4 %copy-start.5 = (bf16[1,128,2560]{2,1,0:T(8,128)(2,1)S(1)}, bf16[1,128,2560]{2,1,0:T(8,128)(2,1)}, u32[]{:S(2)}) copy-start(bf16[1,128,2560]{2,1,0:T(8,128)(2,1)} %param.10) | copy-start | bytes 1966084
  3.5 0.9 copy-start.9
  17.1 0.9 copy-start.2
  18.0 1.2 %copy-start.3 = (bf16[8,128,512]{2,1,0:T(8,128)(2,1)S(1)}, bf16[8,128,512]{2,1,0:T(8,128)(2,1)}, u32[]{:S(2)}) copy-start(bf16[8,128,512]{2,1,0:T(8,128)(2,1)} %get-tuple-element.13.k_ref) | copy-start | bytes 3145732
  19.2 1.2 %copy-start.4 = (bf16[8,128,512]{2,1,0:T(8,128)(2,1)S(1)}, bf16[8,128,512]{2,1,0:T(8,128)(2,1)}, u32[]{:S(2)}) copy-start(bf16[8,128,512]{2,1,0:T(8,128)(2,1)} %get-tuple-element.14.v_ref) | copy-start | bytes 3145732
  20.5 0.7 copy-start.10
  21.2 0.8 copy-start.11
  22.0 7.9 %copy-start.1 = (bf16[1,128,5120]{2,1,0:T(8,128)(2,1)S(1)}, bf16[1,128,5120]{2,1,0:T(8,128)(2,1)}, u32[]{:S(2)}) copy-start(bf16[1,128,5120]{2,1,0:T(8,128)(2,1)} %param.9) | copy-start | bytes 3932164
where the time goes:
time: 103 us
  Pallas kernels  92.1 us (89%)
  local copies, waits for them, and re-layouts  7.31 us (7%)
  matrix products  2.71 us (3%)
    pallas_call x1, Pallas kernels, combine(): pl.pallas_call(functools.partial(combine_kernel, slots, reps, factor), in...  71.5 us
    pallas_call x1, Pallas kernels, share(): pl.pallas_call(functools.partial(share_kernel, slots), in_specs=[anywhere...  12.7 us
    pallas_call x1, Pallas kernels, attention(): pl.pallas_call(attention_kernel, grid=(heads,), in_specs=[smem, smem, pl....  7.89 us
    unnamed x32, local copies, waits for them, and re-layouts  7.31 us

commit v1 on v0

v1 whole, which is shorter than its diff:
```python
import functools
import math

import jax
import jax.numpy as jnp
from jax import lax
from jax.experimental import pallas as pl
from jax.experimental.pallas import tpu as pltpu
from jax.sharding import PartitionSpec as P

KEY_HEADS = 4
HEAD_SIZE = 128
PROMPT = 2
SPAN = 5
STEPS = 1 + PROMPT + SPAN
NEGATIVE = -1e30
F32 = jnp.float32
BF16 = jnp.bfloat16
NT = (((1,), (1,)), ((), ()))
NN = (((1,), (0,)), ((), ()))
TN = (((0,), (0,)), ((), ()))
MESH_ID = pl.DeviceIdType.MESH


def dot(a, b, dims):
    return lax.dot_general(a, b, dims, preferred_element_type=F32)


def split(a):
    high = a.astype(BF16)
    return jnp.concatenate([high, (a - high.astype(F32)).astype(BF16)], axis=1)


def reaches(slot, below):
    return (below > slot) & ((slot < PROMPT) | (below - slot <= SPAN))


def first_pair(own):
    return jnp.maximum((own + 2 * SPAN - SPAN) // 2 - SPAN, 1)


def pair_count(slots):
    most = 1
    for own in range(slots):
        most = max(most, own // 2 - max((own - SPAN) // 2, 1) + 2)
    return most


def peer(node, rep=None):
    target = {"node": node}
    if rep is not None:
        target["rep"] = rep
    return target


def kernel(
    slots, reps, factor,
    parents, lengths, x_ref, q_ref, k_ref, frozen_ref, down_ref, up_ref, g_ref,
    att_ref, qg_ref, down_out, up_out,
    xs, xcat, downs, qs, gs, fs, kbuf, vbuf, lowbuf, score, weight, top, total, inverse, gup,
    atts, qgs, proj, landed, tbuf, upk, upland, parts, gathered, result,
    load_sem, qload, gload, store_a, store_q,
    k_col, k_fwd, k_recv, l_col, l_fwd, l_recv, v_col, v_fwd, v_recv,
    x_send, x_recv, p_send, p_recv, t_send, t_recv, u_send, u_recv,
    r_send, r_recv, a_send, a_recv, b_send, b_recv,
):
    own, rep = lax.axis_index("node"), lax.axis_index("rep")
    heads = qs.shape[0]
    per = heads // KEY_HEADS
    block = qs.shape[1]
    rows = per * block
    width = xs.shape[1]
    half = width // reps
    scale = HEAD_SIZE ** -0.5
    pair = own // 2
    partner = own + 1 - 2 * lax.rem(own, 2)
    pairs = pair - first_pair(own) + 2

    barrier = pltpu.get_barrier_semaphore()
    for step in range(reps):
        other = lax.rem(rep + step, reps)

        def signal(t, carry):
            pl.semaphore_signal(
                barrier, inc=1, device_id=peer(lax.rem(own + t, slots), other),
                device_id_type=MESH_ID,
            )
            return carry

        lax.fori_loop(0 if step else 1, slots, signal, 0)

    def remote(src, dst, send, recv, node, r=None):
        return pltpu.make_async_remote_copy(
            src_ref=src, dst_ref=dst, send_sem=send, recv_sem=recv,
            device_id=peer(node, r), device_id_type=MESH_ID,
        )

    loads = [
        pltpu.make_async_copy(k_ref, kbuf.at[own], load_sem.at[0]),
        pltpu.make_async_copy(down_ref, downs, load_sem.at[1]),
        pltpu.make_async_copy(x_ref, xs, load_sem.at[2]),
        pltpu.make_async_copy(frozen_ref, fs, load_sem.at[3]),
        pltpu.make_async_copy(
            x_ref.at[:, pl.ds(pl.multiple_of(rep * half, 128), half)], xcat.at[rep], load_sem.at[4]
        ),
    ]
    for c in loads:
        c.start()

    def head_copy(source, target, sem, i):
        return pltpu.make_async_copy(
            source.at[:, pl.ds(pl.multiple_of(i * HEAD_SIZE, HEAD_SIZE), HEAD_SIZE)],
            target.at[i], sem.at[i],
        )

    def head_store(source, target, sem, i):
        return pltpu.make_async_copy(
            source.at[i],
            target.at[:, pl.ds(pl.multiple_of(i * HEAD_SIZE, HEAD_SIZE), HEAD_SIZE)],
            sem.at[i],
        )

    def each(low, high, action):
        def body(i, carry):
            action(i)
            return carry

        lax.fori_loop(low, high, body, 0)

    each(0, heads, lambda i: head_copy(q_ref, qs, qload, i).start())
    each(0, heads, lambda i: head_copy(g_ref, gs, gload, i).start())

    chain = []
    current = own
    for _ in range(1, STEPS):
        parent = parents[0, jnp.maximum(current, 0)]
        current = jnp.where(current >= 0, parent, -1)
        chain.append(current)
    own_length = lengths[0, own]

    def limit(slot):
        found = slot == own
        for ancestor in chain:
            found = found | (slot == ancestor)
        return jnp.where(found, lengths[0, slot], 0)

    def unsent(slot):
        same = lax.rem(slot + own, 2) == 0
        lands = same & reaches(slot, 2 * pair) | reaches(slot, own)
        return jnp.logical_not(lands | (slot == own))

    def clear_slot(slot):
        proj[slot] = jnp.zeros(proj.shape[1:], F32)

        @pl.when(unsent(slot))
        def _():
            kbuf[slot] = jnp.zeros(kbuf.shape[1:], BF16)
            vbuf[slot] = jnp.zeros(vbuf.shape[1:], BF16)
            lowbuf[slot] = jnp.zeros(lowbuf.shape[1:], BF16)

    each(0, slots, clear_slot)

    loads[0].wait()
    pl.semaphore_wait(barrier, slots * reps - 1)

    def column(buf, send, recv, t):
        return remote(buf.at[own], buf.at[own], send.at[t], recv.at[own], own + 2 * t)

    def across(buf, send, recv, slot):
        return remote(buf.at[slot], buf.at[slot], send.at[slot], recv.at[slot], partner)

    def columns(action):
        def body(step):
            t = slots // 2 - 1 - step

            @pl.when((own + 2 * t < slots) & reaches(own, 2 * (pair + t)))
            def _():
                action(t)

        each(0, slots // 2 - 1, body)

    def own_across(action):
        @pl.when(reaches(own, partner))
        def _():
            action(own)

    def relayed(action):
        def body(t):
            slot = own - 2 * t

            @pl.when(reaches(slot, 2 * pair))
            def _():
                action(slot)

        each(1, pair + 1, body)

    def forward(buf, send, recv):
        def act(slot):
            across(buf, send, recv, slot).wait_recv()

            @pl.when(reaches(slot, partner))
            def _():
                across(buf, send, recv, slot).start()

        relayed(act)

    def from_partner(buf, send, recv, t):
        slot = partner - 2 * t

        @pl.when(reaches(slot, own))
        def _():
            across(buf, send, recv, slot).wait_recv()

    def send_own(buf, col, fwd, recv):
        own_across(lambda slot: across(buf, fwd, recv, slot).start())
        columns(lambda t: column(buf, col, recv, t).start())

    def drain(buf, col, fwd, recv):
        own_across(lambda slot: across(buf, fwd, recv, slot).wait_send())
        columns(lambda t: column(buf, col, recv, t).wait_send())

        def act(slot):
            @pl.when(reaches(slot, partner))
            def _():
                across(buf, fwd, recv, slot).wait_send()

        relayed(act)

    send_own(kbuf, k_col, k_fwd, k_recv)

    def swap_x(r):
        return remote(
            x_ref.at[:, pl.ds(pl.multiple_of(r * half, 128), half)], xcat.at[rep],
            x_send.at[r], x_recv.at[rep], own, r,
        )

    def other_reps(action):
        for step in range(1, reps):
            action(lax.rem(rep + step, reps))

    other_reps(lambda r: swap_x(r).start())

    loads[1].wait()
    loads[2].wait()
    low = dot(xs[...], downs[...], NN)
    lowbuf[own] = low.T.astype(BF16)
    loads[3].wait()
    vbuf[own] = (fs[...].astype(F32) + dot(low.astype(BF16), up_ref[...], NN)).astype(BF16)
    send_own(lowbuf, l_col, l_fwd, l_recv)
    send_own(vbuf, v_col, v_fwd, v_recv)

    each(0, heads, lambda i: head_copy(q_ref, qs, qload, i).wait())
    each(0, heads, lambda i: head_copy(g_ref, gs, gload, i).wait())

    def stacked(buf, kk):
        return buf[pl.ds(kk * per, per)].reshape(rows, HEAD_SIZE)

    def pair_at(step):
        return jnp.where(step == pairs - 1, 0, pair - step)

    def two(buf, index, kk):
        lanes = pl.ds(pl.multiple_of(kk * HEAD_SIZE, HEAD_SIZE), HEAD_SIZE)
        return buf[pl.ds(2 * index, 2), :, lanes].reshape(2 * block, HEAD_SIZE)

    for kk in range(KEY_HEADS):
        lanes = slice(kk * HEAD_SIZE, (kk + 1) * HEAD_SIZE)
        gup[kk] = dot(stacked(gs, kk), up_ref[:, lanes], NT)

    forward(kbuf, k_fwd, k_recv)
    forward(lowbuf, l_fwd, l_recv)

    key = lax.broadcasted_iota(jnp.int32, (block, 2 * block), 1)
    place = lax.rem(key, block)
    query = lax.broadcasted_iota(jnp.int32, (block, 2 * block), 0)

    def scores(step, mask, first):
        index = pair_at(step)

        def one(kk):
            s = dot(stacked(qs, kk), two(kbuf, index, kk), NT)
            s = jnp.where(mask, s, NEGATIVE)
            score[kk, step] = s
            most = jnp.maximum(s[:, :block], s[:, block:])
            top[kk] = most if first else jnp.maximum(top[kk], most)

        each(0, KEY_HEADS, one)

    from_partner(kbuf, k_fwd, k_recv, 0)
    even, odd = limit(2 * pair), limit(2 * pair + 1)
    here = jnp.where(key < block, 2 * pair, 2 * pair + 1) == own
    mask = (place < jnp.where(key < block, even, odd)) & (jnp.logical_not(here) | (place <= query))
    scores(0, jnp.concatenate([mask] * per, axis=0), True)

    def later(t):
        from_partner(kbuf, k_fwd, k_recv, t)
        index = pair - t

        @pl.when((index == 0) | (index >= first_pair(own)))
        def _():
            step = jnp.where(index == 0, pairs - 1, t)
            even, odd = limit(2 * index), limit(2 * index + 1)
            col = lax.broadcasted_iota(jnp.int32, (rows, 2 * block), 1)
            mask = lax.rem(col, block) < jnp.where(col < block, even, odd)
            scores(step, mask, False)

    each(1, pair + 1, later)

    live = (lax.rem(lax.broadcasted_iota(jnp.int32, (rows, 1), 0), block) < own_length).astype(F32)
    rank = proj.shape[1]

    def weigh(kk):
        most = jnp.max(top[kk], axis=1, keepdims=True)
        total[...] = jnp.zeros_like(total)

        def one(step):
            e = jnp.exp2((score[kk, step] - most) * (scale * math.log2(math.e)))
            score[kk, step] = e
            weight[kk, step] = e.astype(BF16)
            total[...] += e[:, :block] + e[:, block:]

        each(0, pairs, one)
        inv = live / jnp.sum(total[...], axis=1, keepdims=True)
        inverse[kk] = jnp.broadcast_to(inv, (rows, HEAD_SIZE))
        sides = split(gup[kk] * inv)

        def project(step):
            index = pair_at(step)
            both = dot(sides, weight[kk, step], TN)
            both = both[:rank] + both[rank:]
            proj[2 * index] += both[:, :block]
            proj[2 * index + 1] += both[:, block:]

        each(0, pairs, project)

    each(0, KEY_HEADS, weigh)

    def scatter(source, target):
        return remote(
            proj.at[target], landed.at[source], p_send.at[target], p_recv.at[source], target
        )

    def ancestors(action):
        def body(t):
            @pl.when(reaches(t, own))
            def _():
                action(t)

        each(0, slots, body)

    def descendants(action):
        def body(t):
            @pl.when(reaches(own, t))
            def _():
                action(t)

        each(0, slots, body)

    ancestors(lambda t: scatter(own, t).start())
    forward(vbuf, v_fwd, v_recv)

    each(0, pair + 1, lambda t: from_partner(lowbuf, l_fwd, l_recv, t))

    def low_weights(kk):
        total[:, :rank] = jnp.zeros((rows, rank), F32)

        def one(step):
            index = pair_at(step)
            lows = jnp.concatenate([lowbuf[2 * index], lowbuf[2 * index + 1]], axis=1)
            total[:, :rank] += dot(weight[kk, step], lows, NT)

        each(0, pairs, one)
        sides = split(total[:, :rank] * inverse[kk][:, :rank])
        both = dot(sides, stacked(gs, kk), TN)
        upk[kk] = both[:rank] + both[rank:]

    each(0, KEY_HEADS, low_weights)
    share = KEY_HEADS // reps

    def swap_up(r):
        return remote(
            upk.at[pl.ds(r * share, share)], upland.at[rep], u_send.at[r], u_recv.at[rep], own, r
        )

    other_reps(lambda r: swap_up(r).start())

    def add_landed(t):
        remote(
            proj.at[t], landed.at[t], p_send.at[t], p_recv.at[t], t
        ).wait_recv()
        proj[own] += landed[t]

    descendants(add_landed)
    tbuf[rep] = proj[own].astype(BF16)

    def swap_total(r):
        return remote(tbuf.at[rep], tbuf.at[rep], t_send.at[r], t_recv.at[rep], own, r)

    other_reps(lambda r: swap_total(r).start())
    loads[4].wait()

    def arrivals(r):
        remote(
            x_ref.at[:, pl.ds(0, half)], xcat.at[r], x_send.at[r], x_recv.at[r], own, r
        ).wait_recv()
        remote(tbuf.at[r], tbuf.at[r], t_send.at[r], t_recv.at[r], own, r).wait_recv()
        remote(
            upk.at[pl.ds(0, share)], upland.at[r], u_send.at[r], u_recv.at[r], own, r
        ).wait_recv()

    other_reps(arrivals)

    projected = jnp.concatenate([tbuf[r] for r in range(reps)], axis=1)
    ups = upk[pl.ds(rep * share, share)]
    for step in range(1, reps):
        ups = ups + upland[lax.rem(rep + step, reps)]
    upland[rep] = ups
    chunks, _, chunk = parts.shape
    up_half = share * HEAD_SIZE
    for j in range(chunks):
        lo, hi = j * chunk, (j + 1) * chunk
        pieces = []
        if lo < half:
            end = min(hi, half)
            pieces.append(dot(projected, xcat[:, :, lo:end].reshape(reps * block, end - lo), NN))
        for h in range(share):
            if lo <= half + h * HEAD_SIZE < hi:
                pieces.append(upland[rep, h])
        filled = sum(p.shape[1] for p in pieces)
        if filled < chunk:
            pieces.append(jnp.zeros((rank, chunk - filled), F32))
        value = pieces[0] if len(pieces) == 1 else jnp.concatenate(pieces, axis=1)
        parts[j] = value.astype(BF16)

    def reduce_copy(source, node):
        return remote(
            parts.at[node], gathered.at[source], r_send.at[node], r_recv.at[source], node
        )

    def others(action):
        each(1, slots, lambda t: action(lax.rem(own + t, slots)))

    def owners(action):
        def body(node):
            @pl.when(node < chunks)
            def _():
                action(node)

        others(body)

    owners(lambda node: reduce_copy(own, node).start())

    def gather_copy(node, owner):
        return remote(
            result.at[rep, owner], result.at[rep, owner], a_send.at[node], a_recv.at[owner], node
        )

    def swap_result(r, owner):
        return remote(
            result.at[rep, owner], result.at[rep, owner], b_send.at[r, owner],
            b_recv.at[rep, owner], own, r,
        )

    @pl.when(own < chunks)
    def _():
        gathered[own] = parts[own]
        others(lambda node: remote(
            parts.at[own], gathered.at[node], r_send.at[node], r_recv.at[node], node
        ).wait_recv())
        acc = lax.fori_loop(
            0, slots, lambda t, a: a + gathered[t].astype(F32), jnp.zeros((rank, chunk), F32)
        )
        result[rep, own] = (acc * factor).astype(BF16)
        others(lambda node: gather_copy(node, own).start())
        other_reps(lambda r: swap_result(r, own).start())

    each(0, pair + 1, lambda t: from_partner(vbuf, v_fwd, v_recv, t))

    def outputs(kk):
        grad = stacked(gs, kk)
        inv = inverse[kk]
        total[...] = jnp.zeros_like(total)

        def attend(step):
            total[...] += dot(weight[kk, step], two(vbuf, pair_at(step), kk), NN)

        each(0, pairs, attend)
        out = total[...] * inv
        atts[pl.ds(kk * per, per)] = out.astype(BF16).reshape(per, block, HEAD_SIZE)
        dots = jnp.sum(grad.astype(F32) * out, axis=1, keepdims=True)
        slope = inv[:, :1] * scale
        total[...] = jnp.zeros_like(total)

        def back(step):
            index = pair_at(step)
            pressure = dot(grad, two(vbuf, index, kk), NT)
            slopes = (score[kk, step] * ((pressure - dots) * slope)).astype(BF16)
            total[...] += dot(slopes, two(kbuf, index, kk), NN)

        each(0, pairs, back)
        qgs[pl.ds(kk * per, per)] = total[...].astype(BF16).reshape(per, block, HEAD_SIZE)

        def store(i):
            head_store(atts, att_ref, store_a, i).start()
            head_store(qgs, qg_ref, store_q, i).start()

        each(kk * per, (kk + 1) * per, store)

    each(0, KEY_HEADS, outputs)

    def pass_on(owner):
        remote(
            result.at[rep, owner], result.at[rep, owner], a_send.at[owner], a_recv.at[owner], owner
        ).wait_recv()
        other_reps(lambda r: swap_result(r, owner).start())

    owners(pass_on)

    def from_reps(r):
        each(0, chunks, lambda owner: remote(
            result.at[r, owner], result.at[r, owner], b_send.at[r, owner], b_recv.at[r, owner],
            own, r,
        ).wait_recv())

    other_reps(from_reps)
    for r in range(reps):
        for j in range(chunks):
            lo, hi = j * chunk, (j + 1) * chunk
            if lo < half:
                end = min(hi, half)
                down_out[:, r * half + lo:r * half + end] = result[r, j, :, :end - lo].astype(F32)
            if hi > half and lo < half + up_half:
                a, b = max(lo, half), min(hi, half + up_half)
                base = r * up_half - half
                up_out[:, base + a:base + b] = result[r, j, :, a - lo:b - lo].astype(F32)

    drain(kbuf, k_col, k_fwd, k_recv)
    drain(lowbuf, l_col, l_fwd, l_recv)
    drain(vbuf, v_col, v_fwd, v_recv)
    other_reps(lambda r: swap_x(r).wait_send())
    ancestors(lambda t: scatter(own, t).wait_send())
    other_reps(lambda r: swap_up(r).wait_send())
    other_reps(lambda r: swap_total(r).wait_send())
    owners(lambda node: reduce_copy(own, node).wait_send())

    @pl.when(own < chunks)
    def _():
        others(lambda node: gather_copy(node, own).wait_send())

    other_reps(lambda r: each(0, chunks, lambda owner: swap_result(r, owner).wait_send()))
    each(0, heads, lambda i: head_store(atts, att_ref, store_a, i).wait())
    each(0, heads, lambda i: head_store(qgs, qg_ref, store_q, i).wait())


def on_device(x, q, k, frozen, down, up, g, parents, lengths):
    x, q, k, frozen, g = x[0], q[0], k[0], frozen[0], g[0]
    block, width = x.shape
    slots, reps = lax.axis_size("node"), lax.axis_size("rep")
    rank, up_width = up.shape
    heads = q.shape[1] // HEAD_SIZE
    rows = heads // KEY_HEADS * block
    pairs = pair_count(slots)
    tiles = -(-(width + up_width) // reps // 128)
    per = -(-tiles // slots)
    chunks = -(-tiles // per)
    chunk = per * 128
    factor = (slots * reps * block) ** -0.5
    anywhere = pl.BlockSpec(memory_space=pl.ANY)
    vmem = pl.BlockSpec(memory_space=pltpu.VMEM)
    smem = pl.BlockSpec(memory_space=pltpu.SMEM)
    dma = pltpu.SemaphoreType.DMA
    v = pltpu.VMEM
    share = KEY_HEADS // reps
    attended, query_grad, down_sum, up_sum = pl.pallas_call(
        functools.partial(kernel, slots, reps, factor),
        in_specs=[smem, smem, anywhere, anywhere, anywhere, anywhere, anywhere, vmem, anywhere],
        out_specs=[anywhere, anywhere, vmem, vmem],
        out_shape=[
            jax.ShapeDtypeStruct(q.shape, BF16),
            jax.ShapeDtypeStruct(q.shape, BF16),
            jax.ShapeDtypeStruct((rank, width), F32),
            jax.ShapeDtypeStruct((rank, up_width), F32),
        ],
        scratch_shapes=[
            v(x.shape, BF16), v((reps, block, width // reps), BF16), v(down.shape, BF16),
            v((heads, block, HEAD_SIZE), BF16), v((heads, block, HEAD_SIZE), BF16),
            v(frozen.shape, BF16),
            v((slots, block, up_width), BF16), v((slots, block, up_width), BF16),
            v((slots, rank, block), BF16),
            v((KEY_HEADS, pairs, rows, 2 * block), F32),
            v((KEY_HEADS, pairs, rows, 2 * block), BF16),
            v((KEY_HEADS, rows, block), F32), v((rows, HEAD_SIZE), F32),
            v((KEY_HEADS, rows, HEAD_SIZE), F32), v((KEY_HEADS, rows, rank), F32),
            v((heads, block, HEAD_SIZE), BF16), v((heads, block, HEAD_SIZE), BF16),
            v((slots, rank, block), F32), v((slots, rank, block), F32),
            v((reps, rank, block), BF16),
            v((KEY_HEADS, rank, HEAD_SIZE), F32), v((reps, share, rank, HEAD_SIZE), F32),
            v((chunks, rank, chunk), BF16), v((slots, rank, chunk), BF16),
            v((reps, chunks, rank, chunk), BF16),
            dma((5,)), dma((heads,)), dma((heads,)), dma((heads,)), dma((heads,)),
            dma((slots,)), dma((slots,)), dma((slots,)),
            dma((slots,)), dma((slots,)), dma((slots,)),
            dma((slots,)), dma((slots,)), dma((slots,)),
            dma((reps,)), dma((reps,)), dma((slots,)), dma((slots,)),
            dma((reps,)), dma((reps,)), dma((reps,)), dma((reps,)),
            dma((slots,)), dma((slots,)), dma((slots,)), dma((slots,)),
            dma((reps, chunks)), dma((reps, chunks)),
        ],
        compiler_params=pltpu.CompilerParams(
            collective_id=0, has_side_effects=True, vmem_limit_bytes=60 * 1024 * 1024
        ),
        name="tree_attention",
    )(parents, lengths, x, q, k, frozen, down, up, g)
    return attended[None], query_grad[None], down_sum.T, up_sum


def solution(mesh):
    rows = P(("groups", "rep"), "node", None)
    table = P(("groups", "rep"), None)
    return jax.shard_map(
        on_device,
        mesh=mesh,
        in_specs=(rows, rows, rows, rows, P(), P(), rows, table, table),
        out_specs=(rows, rows, P("groups", None), P("groups", None)),
        check_vma=False,
    )
```

time: 103 us -> 72.7 us (0.71)
  the two profiles are of different devices: /device:TPU:0 before, /device:TPU:28 now
where the time goes in v1:
time: 72.7 us; the launch traced here: 72.4 us
  Pallas kernels  65.1 us (90%)
  local copies, waits for them, and re-layouts  6.64 us (9%)
    pallas_call x1, Pallas kernels, on_device(): pl.pallas_call(functools.partial(kernel, slots, reps, factor), in_specs=[...  65.1 us
    unnamed x11, local copies, waits for them, and re-layouts  6.64 us

profile of v1, /device:TPU:28, one launch (start us, length us, event | category | flops | bytes accessed | tf_op | source)
XLA Modules:
  0.0 72.4 jit_solution(3913581851958269623)
XLA Ops:
  0.6 2.3 %copy.13.down_ref = bf16[5120,32]{1,0:T(8,128)(2,1)} copy(bf16[5120,32]{0,1:T(8,128)(2,1)} %param.13) | data formatting | bytes 655360 | tf_op args[4]
  2.9 65.1 %tree_attention.1 = (bf16[128,2560]{1,0:T(8,128)(2,1)}, bf16[128,2560]{1,0:T(8,128)(2,1)}, f32[32,5120]{1,0:T(8,128)}, f32[32,512]{1,0:T(8,128)}) custom-call(s32[1,8]{1,0:T(1,128)} %parents.1, s32[1,8]{1,0:T(1,128)} %lengths.1, bf16[128,5120]{1,0:T(8,128)(2,1)} %bitcast.8, bf16[128,2560]{1,0:T(8,128)(2,1)} %bitcast.9, bf16[128,512]{1,0:T(8,128)(2,1)} %bitcast.14, ...), custom_call_target="tpu_custom_call" | custom-call | tf_op jit(solution)/shard_map/tree_attention/pallas_call | solution.py:573
  68.0 0.0 copy-start.1
  68.0 0.0 copy-start
  68.1 2.1 %copy.18 = bf16[1,128,2560]{2,1,0:T(8,128)(2,1)} copy(bf16[1,128,2560]{2,1,0:T(8,128)(2,1)} %bitcast.13) | data formatting | bytes 1310720
  70.1 0.0 copy-done.1
  70.1 0.0 copy-start.2
  70.1 0.8 %copy.19 = bf16[1,128,2560]{2,1,0:T(8,128)(2,1)} copy(bf16[1,128,2560]{2,1,0:T(8,128)(2,1)S(1)} %bitcast.12) | data formatting | bytes 1310720
  71.0 0.0 copy-done
  71.0 0.8 %copy.20 = f32[5120,32]{0,1:T(8,128)} copy(f32[5120,32]{0,1:T(8,128)S(1)} %bitcast.11) | data formatting | bytes 1310720
  71.8 0.0 copy-done.2
  71.8 0.6 copy.21
Async XLA Ops:
  68.0 2.1 %copy-start.1 = (bf16[128,2560]{1,0:T(8,128)(2,1)S(1)}, bf16[128,2560]{1,0:T(8,128)(2,1)}, u32[]{:S(2)}) copy-start(bf16[128,2560]{1,0:T(8,128)(2,1)} %get-tuple-element.9) | copy-start | bytes 1966084
  68.0 2.9 %copy-start = (f32[32,5120]{1,0:T(8,128)S(1)}, f32[32,5120]{1,0:T(8,128)}, u32[]{:S(2)}) copy-start(f32[32,5120]{1,0:T(8,128)} %get-tuple-element.10) | copy-start | bytes 1966084
  70.1 1.7 %copy-start.2 = (f32[32,512]{1,0:T(8,128)S(1)}, f32[32,512]{1,0:T(8,128)}, u32[]{:S(2)}) copy-start(f32[32,512]{1,0:T(8,128)} %get-tuple-element.19) | copy-start | bytes 196612

commit v2 on v1

--- a/solution.py
+++ b/solution.py
@@ -56,9 +56,9 @@
 def kernel(
     slots, reps, factor,
     parents, lengths, x_ref, q_ref, k_ref, frozen_ref, down_ref, up_ref, g_ref,
-    att_ref, qg_ref, down_out, up_out,
-    xs, xcat, downs, qs, gs, fs, kbuf, vbuf, lowbuf, score, weight, top, total, inverse, gup,
-    atts, qgs, proj, landed, tbuf, upk, upland, parts, gathered, result,
+    att_ref, qg_ref, result,
+    xs, xcat, downs, qs, gs, fs, kbuf, vbuf, lowbuf, score, weight, tops, facs, total, gup,
+    atts, qgs, proj, landed, tbuf, upk, upland, parts, gathered,
     load_sem, qload, gload, store_a, store_q,
     k_col, k_fwd, k_recv, l_col, l_fwd, l_recv, v_col, v_fwd, v_recv,
     x_send, x_recv, p_send, p_recv, t_send, t_recv, u_send, u_recv,
@@ -194,15 +194,16 @@
 
         each(1, pair + 1, body)
 
-    def forward(buf, send, recv):
-        def act(slot):
+    def forward(buf, send, recv, t):
+        slot = own - 2 * t
+
+        @pl.when((t <= pair) & reaches(slot, 2 * pair))
+        def _():
             across(buf, send, recv, slot).wait_recv()
 
             @pl.when(reaches(slot, partner))
             def _():
                 across(buf, send, recv, slot).start()
-
-        relayed(act)
 
     def from_partner(buf, send, recv, t):
         slot = partner - 2 * t
@@ -242,12 +243,11 @@
 
     loads[1].wait()
     loads[2].wait()
-    low = dot(xs[...], downs[...], NN)
-    lowbuf[own] = low.T.astype(BF16)
+    low = dot(downs[...], xs[...], NT).astype(BF16)
+    lowbuf[own] = low
     loads[3].wait()
-    vbuf[own] = (fs[...].astype(F32) + dot(low.astype(BF16), up_ref[...], NN)).astype(BF16)
+    vbuf[own] = (fs[...].astype(F32) + dot(low, up_ref[...], TN)).astype(BF16)
     send_own(lowbuf, l_col, l_fwd, l_recv)
-    send_own(vbuf, v_col, v_fwd, v_recv)
 
     each(0, heads, lambda i: head_copy(q_ref, qs, qload, i).wait())
     each(0, heads, lambda i: head_copy(g_ref, gs, gload, i).wait())
@@ -266,32 +266,46 @@
         lanes = slice(kk * HEAD_SIZE, (kk + 1) * HEAD_SIZE)
         gup[kk] = dot(stacked(gs, kk), up_ref[:, lanes], NT)
 
-    forward(kbuf, k_fwd, k_recv)
-    forward(lowbuf, l_fwd, l_recv)
+    tune = scale * math.log2(math.e)
+    rank = proj.shape[1]
+
+    def wide(column):
+        return jnp.broadcast_to(column, (rows, HEAD_SIZE))
+
+    def scores(step, mask, first):
+        index = pair_at(step)
+
+        def one(kk):
+            s = dot(stacked(qs, kk), two(kbuf, index, kk), NT)
+            s = jnp.where(mask, s, NEGATIVE)
+            most = jnp.max(jnp.maximum(s[:, :block], s[:, block:]), axis=1, keepdims=True)
+            if not first:
+                most = jnp.maximum(most, tops[kk, step - 1][:, :1])
+            e = jnp.exp2((s - most) * tune)
+            score[kk, step] = e
+            weight[kk, step] = e.astype(BF16)
+            tops[kk, step] = wide(most)
+            facs[kk, step] = wide(jnp.sum(e[:, :block] + e[:, block:], axis=1, keepdims=True))
+
+        each(0, KEY_HEADS, one)
 
     key = lax.broadcasted_iota(jnp.int32, (block, 2 * block), 1)
     place = lax.rem(key, block)
     query = lax.broadcasted_iota(jnp.int32, (block, 2 * block), 0)
-
-    def scores(step, mask, first):
-        index = pair_at(step)
-
-        def one(kk):
-            s = dot(stacked(qs, kk), two(kbuf, index, kk), NT)
-            s = jnp.where(mask, s, NEGATIVE)
-            score[kk, step] = s
-            most = jnp.maximum(s[:, :block], s[:, block:])
-            top[kk] = most if first else jnp.maximum(top[kk], most)
-
-        each(0, KEY_HEADS, one)
-
+    forward(kbuf, k_fwd, k_recv, 1)
     from_partner(kbuf, k_fwd, k_recv, 0)
     even, odd = limit(2 * pair), limit(2 * pair + 1)
     here = jnp.where(key < block, 2 * pair, 2 * pair + 1) == own
     mask = (place < jnp.where(key < block, even, odd)) & (jnp.logical_not(here) | (place <= query))
     scores(0, jnp.concatenate([mask] * per, axis=0), True)
+    forward(kbuf, k_fwd, k_recv, 2)
+    send_own(vbuf, v_col, v_fwd, v_recv)
 
     def later(t):
+        @pl.when(t == pair)
+        def _():
+            forward(vbuf, v_fwd, v_recv, 1)
+
         from_partner(kbuf, k_fwd, k_recv, t)
         index = pair - t
 
@@ -303,29 +317,29 @@
             mask = lax.rem(col, block) < jnp.where(col < block, even, odd)
             scores(step, mask, False)
 
+        forward(kbuf, k_fwd, k_recv, t + 2)
+
     each(1, pair + 1, later)
 
     live = (lax.rem(lax.broadcasted_iota(jnp.int32, (rows, 1), 0), block) < own_length).astype(F32)
-    rank = proj.shape[1]
 
     def weigh(kk):
-        most = jnp.max(top[kk], axis=1, keepdims=True)
+        most = tops[kk, pairs - 1]
         total[...] = jnp.zeros_like(total)
 
-        def one(step):
-            e = jnp.exp2((score[kk, step] - most) * (scale * math.log2(math.e)))
-            score[kk, step] = e
-            weight[kk, step] = e.astype(BF16)
-            total[...] += e[:, :block] + e[:, block:]
-
-        each(0, pairs, one)
-        inv = live / jnp.sum(total[...], axis=1, keepdims=True)
-        inverse[kk] = jnp.broadcast_to(inv, (rows, HEAD_SIZE))
-        sides = split(gup[kk] * inv)
+        def add(step):
+            fall = jnp.exp2((tops[kk, step] - most) * tune)
+            total[...] += facs[kk, step] * fall
+            facs[kk, step] = fall
+
+        each(0, pairs, add)
+        total[...] = live / total[...]
 
         def project(step):
             index = pair_at(step)
-            both = dot(sides, weight[kk, step], TN)
+            fac = facs[kk, step] * total[...]
+            facs[kk, step] = fac
+            both = dot(split(gup[kk] * fac[:, :rank]), weight[kk, step], TN)
             both = both[:rank] + both[rank:]
             proj[2 * index] += both[:, :block]
             proj[2 * index + 1] += both[:, block:]
@@ -356,8 +370,8 @@
         each(0, slots, body)
 
     ancestors(lambda t: scatter(own, t).start())
-    forward(vbuf, v_fwd, v_recv)
-
+    each(1, pair + 1, lambda t: forward(lowbuf, l_fwd, l_recv, t))
+    each(2, pair + 1, lambda t: forward(vbuf, v_fwd, v_recv, t))
     each(0, pair + 1, lambda t: from_partner(lowbuf, l_fwd, l_recv, t))
 
     def low_weights(kk):
@@ -366,10 +380,10 @@
         def one(step):
             index = pair_at(step)
             lows = jnp.concatenate([lowbuf[2 * index], lowbuf[2 * index + 1]], axis=1)
-            total[:, :rank] += dot(weight[kk, step], lows, NT)
+            total[:, :rank] += dot(weight[kk, step], lows, NT) * facs[kk, step][:, :rank]
 
         each(0, pairs, one)
-        sides = split(total[:, :rank] * inverse[kk][:, :rank])
+        sides = split(total[:, :rank])
         both = dot(sides, stacked(gs, kk), TN)
         upk[kk] = both[:rank] + both[rank:]
 
@@ -415,7 +429,6 @@
         ups = ups + upland[lax.rem(rep + step, reps)]
     upland[rep] = ups
     chunks, _, chunk = parts.shape
-    up_half = share * HEAD_SIZE
     for j in range(chunks):
         lo, hi = j * chunk, (j + 1) * chunk
         pieces = []
@@ -449,6 +462,40 @@
 
     owners(lambda node: reduce_copy(own, node).start())
 
+    each(0, pair + 1, lambda t: from_partner(vbuf, v_fwd, v_recv, t))
+
+    def outputs(kk):
+        grad = stacked(gs, kk)
+        total[...] = jnp.zeros_like(total)
+
+        def attend(step):
+            total[...] += dot(weight[kk, step], two(vbuf, pair_at(step), kk), NN) * facs[kk, step]
+
+        each(0, pairs, attend)
+        out = total[...]
+        atts[pl.ds(kk * per, per)] = out.astype(BF16).reshape(per, block, HEAD_SIZE)
+        dots = jnp.sum(grad.astype(F32) * out, axis=1, keepdims=True)
+        total[...] = jnp.zeros_like(total)
+
+        def back(step):
+            index = pair_at(step)
+            pressure = dot(grad, two(vbuf, index, kk), NT)
+            slope = facs[kk, step] * scale
+            slopes = (score[kk, step] * ((pressure - dots) * jnp.concatenate([slope, slope], axis=1))).astype(BF16)
+            total[...] += dot(slopes, two(kbuf, index, kk), NN)
+
+        each(0, pairs, back)
+        qgs[pl.ds(kk * per, per)] = total[...].astype(BF16).reshape(per, block, HEAD_SIZE)
+
+        def store(i):
+            head_store(atts, att_ref, store_a, i).start()
+            head_store(qgs, qg_ref, store_q, i).start()
+
+        each(kk * per, (kk + 1) * per, store)
+
+    outputs_early = 1
+    each(0, outputs_early, outputs)
+
     def gather_copy(node, owner):
         return remote(
             result.at[rep, owner], result.at[rep, owner], a_send.at[node], a_recv.at[owner], node
@@ -473,39 +520,7 @@
         others(lambda node: gather_copy(node, own).start())
         other_reps(lambda r: swap_result(r, own).start())
 
-    each(0, pair + 1, lambda t: from_partner(vbuf, v_fwd, v_recv, t))
-
-    def outputs(kk):
-        grad = stacked(gs, kk)
-        inv = inverse[kk]
-        total[...] = jnp.zeros_like(total)
-
-        def attend(step):
-            total[...] += dot(weight[kk, step], two(vbuf, pair_at(step), kk), NN)
-
-        each(0, pairs, attend)
-        out = total[...] * inv
-        atts[pl.ds(kk * per, per)] = out.astype(BF16).reshape(per, block, HEAD_SIZE)
-        dots = jnp.sum(grad.astype(F32) * out, axis=1, keepdims=True)
-        slope = inv[:, :1] * scale
-        total[...] = jnp.zeros_like(total)
-
-        def back(step):
-            index = pair_at(step)
-            pressure = dot(grad, two(vbuf, index, kk), NT)
-            slopes = (score[kk, step] * ((pressure - dots) * slope)).astype(BF16)
-            total[...] += dot(slopes, two(kbuf, index, kk), NN)
-
-        each(0, pairs, back)
-        qgs[pl.ds(kk * per, per)] = total[...].astype(BF16).reshape(per, block, HEAD_SIZE)
-
-        def store(i):
-            head_store(atts, att_ref, store_a, i).start()
-            head_store(qgs, qg_ref, store_q, i).start()
-
-        each(kk * per, (kk + 1) * per, store)
-
-    each(0, KEY_HEADS, outputs)
+    each(outputs_early, KEY_HEADS, outputs)
 
     def pass_on(owner):
         remote(
@@ -522,17 +537,6 @@
         ).wait_recv())
 
     other_reps(from_reps)
-    for r in range(reps):
-        for j in range(chunks):
-            lo, hi = j * chunk, (j + 1) * chunk
-            if lo < half:
-                end = min(hi, half)
-                down_out[:, r * half + lo:r * half + end] = result[r, j, :, :end - lo].astype(F32)
-            if hi > half and lo < half + up_half:
-                a, b = max(lo, half), min(hi, half + up_half)
-                base = r * up_half - half
-                up_out[:, base + a:base + b] = result[r, j, :, a - lo:b - lo].astype(F32)
-
     drain(kbuf, k_col, k_fwd, k_recv)
     drain(lowbuf, l_col, l_fwd, l_recv)
     drain(vbuf, v_col, v_fwd, v_recv)
@@ -549,6 +553,50 @@
     other_reps(lambda r: each(0, chunks, lambda owner: swap_result(r, owner).wait_send()))
     each(0, heads, lambda i: head_store(atts, att_ref, store_a, i).wait())
     each(0, heads, lambda i: head_store(qgs, qg_ref, store_q, i).wait())
+
+
+def finish(cuts, a_ref, b_ref, r_ref, att_ref, qg_ref, down_ref, up_ref, a, b, res, down, up, ins, outs, sems):
+    step = a_ref.shape[0] // cuts
+
+    def move(i, source, target, sem, part):
+        at = pl.ds(part * step, step)
+        return pltpu.make_async_copy(source.at[at], target.at[at], sem.at[i, part])
+
+    load = pltpu.make_async_copy(r_ref, res, sems.at[0])
+    load.start()
+    pieces = [(0, a_ref, a, att_ref), (1, b_ref, b, qg_ref)]
+    for part in range(cuts):
+        for i, source, buf, _ in pieces:
+            move(i, source, buf, ins, part).start()
+    load.wait()
+    reps, chunks, rank, chunk = res.shape
+    half = down.shape[1] // reps
+    up_half = up.shape[1] // reps
+    for r in range(reps):
+        for j in range(chunks):
+            lo, hi = j * chunk, (j + 1) * chunk
+            if lo < half:
+                end = min(hi, half)
+                down[:, r * half + lo:r * half + end] = res[r, j, :, :end - lo].astype(F32)
+            if hi > half and lo < half + up_half:
+                first, last = max(lo, half), min(hi, half + up_half)
+                base = r * up_half - half
+                up[:, base + first:base + last] = res[r, j, :, first - lo:last - lo].astype(F32)
+    stores = [
+        pltpu.make_async_copy(down, down_ref, sems.at[1]),
+        pltpu.make_async_copy(up, up_ref, sems.at[2]),
+    ]
+    for c in stores:
+        c.start()
+    for part in range(cuts):
+        for i, source, buf, target in pieces:
+            move(i, source, buf, ins, part).wait()
+            move(i, buf, target, outs, part).start()
+    for part in range(cuts):
+        for i, source, buf, target in pieces:
+            move(i, buf, target, outs, part).wait()
+    for c in stores:
+        c.wait()
 
 
 def on_device(x, q, k, frozen, down, up, g, parents, lengths):
@@ -570,32 +618,30 @@
     dma = pltpu.SemaphoreType.DMA
     v = pltpu.VMEM
     share = KEY_HEADS // reps
-    attended, query_grad, down_sum, up_sum = pl.pallas_call(
+    attended, query_grad, result = pl.pallas_call(
         functools.partial(kernel, slots, reps, factor),
         in_specs=[smem, smem, anywhere, anywhere, anywhere, anywhere, anywhere, vmem, anywhere],
-        out_specs=[anywhere, anywhere, vmem, vmem],
+        out_specs=[anywhere, anywhere, vmem],
         out_shape=[
             jax.ShapeDtypeStruct(q.shape, BF16),
             jax.ShapeDtypeStruct(q.shape, BF16),
-            jax.ShapeDtypeStruct((rank, width), F32),
-            jax.ShapeDtypeStruct((rank, up_width), F32),
+            jax.ShapeDtypeStruct((reps, chunks, rank, chunk), BF16),
         ],
         scratch_shapes=[
-            v(x.shape, BF16), v((reps, block, width // reps), BF16), v(down.shape, BF16),
+            v(x.shape, BF16), v((reps, block, width // reps), BF16), v((rank, width), BF16),
             v((heads, block, HEAD_SIZE), BF16), v((heads, block, HEAD_SIZE), BF16),
             v(frozen.shape, BF16),
             v((slots, block, up_width), BF16), v((slots, block, up_width), BF16),
             v((slots, rank, block), BF16),
             v((KEY_HEADS, pairs, rows, 2 * block), F32),
             v((KEY_HEADS, pairs, rows, 2 * block), BF16),
-            v((KEY_HEADS, rows, block), F32), v((rows, HEAD_SIZE), F32),
-            v((KEY_HEADS, rows, HEAD_SIZE), F32), v((KEY_HEADS, rows, rank), F32),
+            v((KEY_HEADS, pairs, rows, HEAD_SIZE), F32), v((KEY_HEADS, pairs, rows, HEAD_SIZE), F32),
+            v((rows, HEAD_SIZE), F32), v((KEY_HEADS, rows, rank), F32),
             v((heads, block, HEAD_SIZE), BF16), v((heads, block, HEAD_SIZE), BF16),
             v((slots, rank, block), F32), v((slots, rank, block), F32),
             v((reps, rank, block), BF16),
             v((KEY_HEADS, rank, HEAD_SIZE), F32), v((reps, share, rank, HEAD_SIZE), F32),
             v((chunks, rank, chunk), BF16), v((slots, rank, chunk), BF16),
-            v((reps, chunks, rank, chunk), BF16),
             dma((5,)), dma((heads,)), dma((heads,)), dma((heads,)), dma((heads,)),
             dma((slots,)), dma((slots,)), dma((slots,)),
             dma((slots,)), dma((slots,)), dma((slots,)),
@@ -609,7 +655,26 @@
             collective_id=0, has_side_effects=True, vmem_limit_bytes=60 * 1024 * 1024
         ),
         name="tree_attention",
-    )(parents, lengths, x, q, k, frozen, down, up, g)
+    )(parents, lengths, x, q, k, frozen, down.T, up, g)
+    cuts = 2
+    attended, query_grad, down_sum, up_sum = pl.pallas_call(
+        functools.partial(finish, cuts),
+        in_specs=[anywhere, anywhere, anywhere],
+        out_specs=[anywhere, anywhere, anywhere, anywhere],
+        out_shape=[
+            jax.ShapeDtypeStruct(q.shape, BF16),
+            jax.ShapeDtypeStruct(q.shape, BF16),
+            jax.ShapeDtypeStruct((rank, width), F32),
+            jax.ShapeDtypeStruct((rank, up_width), F32),
+        ],
+        scratch_shapes=[
+            v(q.shape, BF16), v(q.shape, BF16), v(result.shape, BF16),
+            v((rank, width), F32), v((rank, up_width), F32),
+            dma((2, cuts)), dma((2, cuts)), dma((3,)),
+        ],
+        compiler_params=pltpu.CompilerParams(vmem_limit_bytes=60 * 1024 * 1024),
+        name="finish",
+    )(attended, query_grad, result)
     return attended[None], query_grad[None], down_sum.T, up_sum
 
 

time: 72.7 us -> 68.6 us (0.944)
  the two profiles are of different devices: /device:TPU:28 before, /device:TPU:0 now
where the time goes in v2:
time: 68.6 us; the launch traced here: 68 us
  Pallas kernels  67.4 us (98%)
    pallas_call x1, Pallas kernels, on_device(): pl.pallas_call(functools.partial(kernel, slots, reps, factor), in_specs=[...  64.6 us
    pallas_call x1, Pallas kernels, on_device(): pl.pallas_call(functools.partial(finish, cuts), in_specs=[anywhere, anywh...  2.72 us

profile of v2, /device:TPU:0, one launch (start us, length us, event | category | flops | bytes accessed | tf_op | source)
XLA Modules:
  0.0 68.0 jit_solution(10415560855430068066)
XLA Ops:
  0.6 64.6 %tree_attention.1 = (bf16[128,2560]{1,0:T(8,128)(2,1)}, bf16[128,2560]{1,0:T(8,128)(2,1)}, bf16[2,8,32,384]{3,2,1,0:T(8,128)(2,1)}) custom-call(s32[1,8]{1,0:T(1,128)} %parents.1, s32[1,8]{1,0:T(1,128)} %lengths.1, bf16[128,5120]{1,0:T(8,128)(2,1)} %bitcast.9, bf16[128,2560]{1,0:T(8,128)(2,1)} %bitcast.10, bf16[128,512]{1,0:T(8,128)(2,1)} %bitcast.13, ...), custom_call_target="tpu_custom_call" | custom-call | tf_op jit(solution)/shard_map/tree_attention/pallas_call | solution.py:621
  65.3 2.7 %finish.1 = (bf16[128,2560]{1,0:T(8,128)(2,1)}, bf16[128,2560]{1,0:T(8,128)(2,1)}, f32[32,5120]{1,0:T(8,128)}, f32[32,512]{1,0:T(8,128)}) custom-call(bf16[128,2560]{1,0:T(8,128)(2,1)} %get-tuple-element.11.a_ref, bf16[128,2560]{1,0:T(8,128)(2,1)} %get-tuple-element.12.b_ref, bf16[2,8,32,384]{3,2,1,0:T(8,128)(2,1)} %get-tuple-element.13.r_ref), custom_call_target="tpu_custom_call" | custom-call | tf_op jit(solution)/shard_map/finish/pallas_call | solution.py:660

commit v3 on v2

--- a/solution.py
+++ b/solution.py
@@ -26,11 +26,6 @@
     return lax.dot_general(a, b, dims, preferred_element_type=F32)
 
 
-def split(a):
-    high = a.astype(BF16)
-    return jnp.concatenate([high, (a - high.astype(F32)).astype(BF16)], axis=1)
-
-
 def reaches(slot, below):
     return (below > slot) & ((slot < PROMPT) | (below - slot <= SPAN))
 
@@ -57,9 +52,9 @@
     slots, reps, factor,
     parents, lengths, x_ref, q_ref, k_ref, frozen_ref, down_ref, up_ref, g_ref,
     att_ref, qg_ref, result,
-    xs, xcat, downs, qs, gs, fs, kbuf, vbuf, lowbuf, score, weight, tops, facs, total, gup,
-    atts, qgs, proj, landed, tbuf, upk, upland, parts, gathered,
-    load_sem, qload, gload, store_a, store_q,
+    xs, xcat, downs, qs, gs, fs, kbuf, vbuf, lowbuf, score, weight, tops, facs, acc, gup, gtr,
+    vgrad, both, atts, qgs, proj, landed, tbuf, upk, upland, parts, gathered,
+    load_sem, kload, qload, gload, store_a, store_q,
     k_col, k_fwd, k_recv, l_col, l_fwd, l_recv, v_col, v_fwd, v_recv,
     x_send, x_recv, p_send, p_recv, t_send, t_recv, u_send, u_recv,
     r_send, r_recv, a_send, a_recv, b_send, b_recv,
@@ -96,14 +91,21 @@
         )
 
     loads = [
-        pltpu.make_async_copy(k_ref, kbuf.at[own], load_sem.at[0]),
         pltpu.make_async_copy(down_ref, downs, load_sem.at[1]),
         pltpu.make_async_copy(x_ref, xs, load_sem.at[2]),
         pltpu.make_async_copy(frozen_ref, fs, load_sem.at[3]),
         pltpu.make_async_copy(
-            x_ref.at[:, pl.ds(pl.multiple_of(rep * half, 128), half)], xcat.at[rep], load_sem.at[4]
+            x_ref.at[:, pl.ds(pl.multiple_of(rep * half, 128), half)], xcat.at[rep], load_sem.at[0]
         ),
     ]
+    def key_load(kk):
+        return pltpu.make_async_copy(
+            k_ref.at[:, pl.ds(pl.multiple_of(kk * HEAD_SIZE, HEAD_SIZE), HEAD_SIZE)],
+            kbuf.at[own, kk], kload.at[kk],
+        )
+
+    for kk in range(KEY_HEADS):
+        key_load(kk).start()
     for c in loads:
         c.start()
 
@@ -160,74 +162,80 @@
 
     each(0, slots, clear_slot)
 
-    loads[0].wait()
+    for kk in range(KEY_HEADS):
+        key_load(kk).wait()
     pl.semaphore_wait(barrier, slots * reps - 1)
 
-    def column(buf, send, recv, t):
-        return remote(buf.at[own], buf.at[own], send.at[t], recv.at[own], own + 2 * t)
-
-    def across(buf, send, recv, slot):
-        return remote(buf.at[slot], buf.at[slot], send.at[slot], recv.at[slot], partner)
-
-    def columns(action):
-        def body(step):
-            t = slots // 2 - 1 - step
-
-            @pl.when((own + 2 * t < slots) & reaches(own, 2 * (pair + t)))
+    class Stream:
+        def __init__(self, buf, col, fwd, recv):
+            self.buf, self.col, self.fwd, self.recv = buf, col, fwd, recv
+
+        def column(self, t, kk):
+            return remote(
+                self.buf.at[own, kk], self.buf.at[own, kk], self.col.at[t, kk],
+                self.recv.at[own, kk], own + 2 * t,
+            )
+
+        def across(self, slot, kk):
+            return remote(
+                self.buf.at[slot, kk], self.buf.at[slot, kk], self.fwd.at[slot, kk],
+                self.recv.at[slot, kk], partner,
+            )
+
+        def own_copies(self, kk, action):
+            @pl.when(reaches(own, partner))
             def _():
-                action(t)
-
-        each(0, slots // 2 - 1, body)
-
-    def own_across(action):
-        @pl.when(reaches(own, partner))
-        def _():
-            action(own)
-
-    def relayed(action):
-        def body(t):
-            slot = own - 2 * t
-
-            @pl.when(reaches(slot, 2 * pair))
+                action(self.across(own, kk))
+
+            def body(step):
+                t = slots // 2 - 1 - step
+
+                @pl.when((own + 2 * t < slots) & reaches(own, 2 * (pair + t)))
+                def _():
+                    action(self.column(t, kk))
+
+            each(0, slots // 2 - 1, body)
+
+        def send(self, kk):
+            self.own_copies(kk, lambda c: c.start())
+
+        def forward(self, kk):
+            def body(t):
+                slot = own - 2 * t
+
+                @pl.when(reaches(slot, 2 * pair))
+                def _():
+                    self.across(slot, kk).wait_recv()
+
+                    @pl.when(reaches(slot, partner))
+                    def _():
+                        self.across(slot, kk).start()
+
+            each(1, pair + 1, body)
+
+        def from_partner(self, t, kk):
+            slot = partner - 2 * t
+
+            @pl.when(reaches(slot, own))
             def _():
-                action(slot)
-
-        each(1, pair + 1, body)
-
-    def forward(buf, send, recv, t):
-        slot = own - 2 * t
-
-        @pl.when((t <= pair) & reaches(slot, 2 * pair))
-        def _():
-            across(buf, send, recv, slot).wait_recv()
-
-            @pl.when(reaches(slot, partner))
-            def _():
-                across(buf, send, recv, slot).start()
-
-    def from_partner(buf, send, recv, t):
-        slot = partner - 2 * t
-
-        @pl.when(reaches(slot, own))
-        def _():
-            across(buf, send, recv, slot).wait_recv()
-
-    def send_own(buf, col, fwd, recv):
-        own_across(lambda slot: across(buf, fwd, recv, slot).start())
-        columns(lambda t: column(buf, col, recv, t).start())
-
-    def drain(buf, col, fwd, recv):
-        own_across(lambda slot: across(buf, fwd, recv, slot).wait_send())
-        columns(lambda t: column(buf, col, recv, t).wait_send())
-
-        def act(slot):
-            @pl.when(reaches(slot, partner))
-            def _():
-                across(buf, fwd, recv, slot).wait_send()
-
-        relayed(act)
-
-    send_own(kbuf, k_col, k_fwd, k_recv)
+                self.across(slot, kk).wait_recv()
+
+        def drain(self, kk):
+            self.own_copies(kk, lambda c: c.wait_send())
+
+            def body(t):
+                slot = own - 2 * t
+
+                @pl.when(reaches(slot, 2 * pair) & reaches(slot, partner))
+                def _():
+                    self.across(slot, kk).wait_send()
+
+            each(1, pair + 1, body)
+
+    keys = Stream(kbuf, k_col, k_fwd, k_recv)
+    values = Stream(vbuf, v_col, v_fwd, v_recv)
+    lows = Stream(lowbuf, l_col, l_fwd, l_recv)
+    each(0, KEY_HEADS, keys.send)
 
     def swap_x(r):
         return remote(
@@ -241,13 +249,15 @@
 
     other_reps(lambda r: swap_x(r).start())
 
+    loads[0].wait()
     loads[1].wait()
+    low = dot(downs[...], xs[...], NT).astype(BF16)
+    lowbuf[own, 0] = low
     loads[2].wait()
-    low = dot(downs[...], xs[...], NT).astype(BF16)
-    lowbuf[own] = low
-    loads[3].wait()
-    vbuf[own] = (fs[...].astype(F32) + dot(low, up_ref[...], TN)).astype(BF16)
-    send_own(lowbuf, l_col, l_fwd, l_recv)
+    own_values = (fs[...].astype(F32) + dot(low, up_ref[...], TN)).astype(BF16)
+    for kk in range(KEY_HEADS):
+        vbuf[own, kk] = own_values[:, kk * HEAD_SIZE:(kk + 1) * HEAD_SIZE]
+    lows.send(0)
 
     each(0, heads, lambda i: head_copy(q_ref, qs, qload, i).wait())
     each(0, heads, lambda i: head_copy(g_ref, gs, gload, i).wait())
@@ -259,94 +269,128 @@
         return jnp.where(step == pairs - 1, 0, pair - step)
 
     def two(buf, index, kk):
-        lanes = pl.ds(pl.multiple_of(kk * HEAD_SIZE, HEAD_SIZE), HEAD_SIZE)
-        return buf[pl.ds(2 * index, 2), :, lanes].reshape(2 * block, HEAD_SIZE)
+        return buf[pl.ds(2 * index, 2), kk].reshape(2 * block, HEAD_SIZE)
 
     for kk in range(KEY_HEADS):
         lanes = slice(kk * HEAD_SIZE, (kk + 1) * HEAD_SIZE)
-        gup[kk] = dot(stacked(gs, kk), up_ref[:, lanes], NT)
+        gup[kk] = dot(up_ref[:, lanes], stacked(gs, kk), NT)
+        for i in range(per):
+            at = slice(i * block, (i + 1) * block)
+            gtr[kk, :, at] = gs[kk * per + i].astype(F32).T.astype(BF16)
 
     tune = scale * math.log2(math.e)
     rank = proj.shape[1]
-
-    def wide(column):
-        return jnp.broadcast_to(column, (rows, HEAD_SIZE))
-
-    def scores(step, mask, first):
-        index = pair_at(step)
-
-        def one(kk):
-            s = dot(stacked(qs, kk), two(kbuf, index, kk), NT)
-            s = jnp.where(mask, s, NEGATIVE)
-            most = jnp.max(jnp.maximum(s[:, :block], s[:, block:]), axis=1, keepdims=True)
-            if not first:
-                most = jnp.maximum(most, tops[kk, step - 1][:, :1])
-            e = jnp.exp2((s - most) * tune)
-            score[kk, step] = e
-            weight[kk, step] = e.astype(BF16)
-            tops[kk, step] = wide(most)
-            facs[kk, step] = wide(jnp.sum(e[:, :block] + e[:, block:], axis=1, keepdims=True))
-
-        each(0, KEY_HEADS, one)
-
-    key = lax.broadcasted_iota(jnp.int32, (block, 2 * block), 1)
-    place = lax.rem(key, block)
-    query = lax.broadcasted_iota(jnp.int32, (block, 2 * block), 0)
-    forward(kbuf, k_fwd, k_recv, 1)
-    from_partner(kbuf, k_fwd, k_recv, 0)
-    even, odd = limit(2 * pair), limit(2 * pair + 1)
-    here = jnp.where(key < block, 2 * pair, 2 * pair + 1) == own
-    mask = (place < jnp.where(key < block, even, odd)) & (jnp.logical_not(here) | (place <= query))
-    scores(0, jnp.concatenate([mask] * per, axis=0), True)
-    forward(kbuf, k_fwd, k_recv, 2)
-    send_own(vbuf, v_col, v_fwd, v_recv)
-
-    def later(t):
-        @pl.when(t == pair)
+    eights = 2 * block // 8
+
+    def times(a, row):
+        return (a.reshape(-1, 8, rows) * row[None]).reshape(a.shape)
+
+    def eight(row):
+        return jnp.broadcast_to(row, (8, rows))
+
+    def scores(kk, step, mask, first):
+        s = dot(two(kbuf, pair_at(step), kk), stacked(qs, kk), NT)
+        s = jnp.where(mask, s, NEGATIVE).reshape(eights, 8, rows)
+        most = eight(jnp.max(jnp.max(s, axis=0), axis=0, keepdims=True))
+        if not first:
+            most = jnp.maximum(most, tops[kk, step - 1])
+        e = jnp.exp2((s - most[None]) * tune)
+        score[kk, step] = e.reshape(2 * block, rows)
+        weight[kk, step] = e.reshape(2 * block, rows).astype(BF16)
+        tops[kk, step] = most
+        facs[kk, step] = eight(jnp.sum(jnp.sum(e, axis=0), axis=0, keepdims=True))
+
+    def seen(index):
+        return limit(2 * index), limit(2 * index + 1)
+
+    def own_pair(kk):
+        keys.from_partner(0, kk)
+        key = lax.broadcasted_iota(jnp.int32, (2 * block, block), 0)
+        place = lax.rem(key, block)
+        query = lax.broadcasted_iota(jnp.int32, (2 * block, block), 1)
+        even, odd = seen(pair)
+        here = jnp.where(key < block, 2 * pair, 2 * pair + 1) == own
+        mask = (place < jnp.where(key < block, even, odd)) & (
+            jnp.logical_not(here) | (place <= query)
+        )
+        scores(kk, 0, jnp.concatenate([mask] * per, axis=1), True)
+
+    def other_pairs(kk):
+        def body(t):
+            keys.from_partner(t, kk)
+            index = pair - t
+
+            @pl.when((index == 0) | (index >= first_pair(own)))
+            def _():
+                even, odd = seen(index)
+                key = lax.broadcasted_iota(jnp.int32, (2 * block, rows), 0)
+                mask = lax.rem(key, block) < jnp.where(key < block, even, odd)
+                scores(kk, jnp.where(index == 0, pairs - 1, t), mask, False)
+
+        each(1, pair + 1, body)
+
+    keys.forward(0)
+
+    def arrive(kk):
+        @pl.when(kk + 1 < KEY_HEADS)
         def _():
-            forward(vbuf, v_fwd, v_recv, 1)
-
-        from_partner(kbuf, k_fwd, k_recv, t)
-        index = pair - t
-
-        @pl.when((index == 0) | (index >= first_pair(own)))
+            keys.forward(kk + 1)
+
+        own_pair(kk)
+
+        @pl.when(kk == 0)
         def _():
-            step = jnp.where(index == 0, pairs - 1, t)
-            even, odd = limit(2 * index), limit(2 * index + 1)
-            col = lax.broadcasted_iota(jnp.int32, (rows, 2 * block), 1)
-            mask = lax.rem(col, block) < jnp.where(col < block, even, odd)
-            scores(step, mask, False)
-
-        forward(kbuf, k_fwd, k_recv, t + 2)
-
-    each(1, pair + 1, later)
-
-    live = (lax.rem(lax.broadcasted_iota(jnp.int32, (rows, 1), 0), block) < own_length).astype(F32)
+            each(0, KEY_HEADS, values.send)
+
+        other_pairs(kk)
+
+    each(0, KEY_HEADS, arrive)
+    values.forward(0)
+    live = (
+        lax.rem(lax.broadcasted_iota(jnp.int32, (8, rows), 1), block) < own_length
+    ).astype(F32)
+
+    def clear_both(step):
+        both[step] = jnp.zeros(both.shape[1:], F32)
+
+    each(0, pairs, clear_both)
 
     def weigh(kk):
         most = tops[kk, pairs - 1]
-        total[...] = jnp.zeros_like(total)
-
-        def add(step):
+
+        def add(step, total):
             fall = jnp.exp2((tops[kk, step] - most) * tune)
-            total[...] += facs[kk, step] * fall
+            total = total + facs[kk, step] * fall
             facs[kk, step] = fall
-
-        each(0, pairs, add)
-        total[...] = live / total[...]
+            return total
+
+        inverse = live / lax.fori_loop(0, pairs, add, jnp.zeros((8, rows), F32))
 
         def project(step):
-            index = pair_at(step)
-            fac = facs[kk, step] * total[...]
+            fac = facs[kk, step] * inverse
             facs[kk, step] = fac
-            both = dot(split(gup[kk] * fac[:, :rank]), weight[kk, step], TN)
-            both = both[:rank] + both[rank:]
-            proj[2 * index] += both[:, :block]
-            proj[2 * index + 1] += both[:, block:]
+            side = times(gup[kk], fac)
+            high = side.astype(BF16)
+            right = jnp.concatenate(
+                [times(gtr[kk].astype(F32), fac).astype(BF16), high,
+                 (side - high.astype(F32)).astype(BF16)], axis=0,
+            )
+            out = dot(weight[kk, step], right, NT)
+            vgrad[kk, step] = out[:, :HEAD_SIZE].astype(BF16)
+            both[step] += out[:, HEAD_SIZE:]
 
         each(0, pairs, project)
 
     each(0, KEY_HEADS, weigh)
+
+    def place(step):
+        index = pair_at(step)
+        turned = both[step].T
+        turned = turned[:rank] + turned[rank:]
+        proj[2 * index] = turned[:, :block]
+        proj[2 * index + 1] = turned[:, block:]
+
+    each(0, pairs, place)
 
     def scatter(source, target):
         return remote(
@@ -370,24 +414,23 @@
         each(0, slots, body)
 
     ancestors(lambda t: scatter(own, t).start())
-    each(1, pair + 1, lambda t: forward(lowbuf, l_fwd, l_recv, t))
-    each(2, pair + 1, lambda t: forward(vbuf, v_fwd, v_recv, t))
-    each(0, pair + 1, lambda t: from_partner(lowbuf, l_fwd, l_recv, t))
+    lows.forward(0)
+    values.forward(1)
+    values.forward(2)
+    each(0, pair + 1, lambda t: lows.from_partner(t, 0))
 
     def low_weights(kk):
-        total[:, :rank] = jnp.zeros((rows, rank), F32)
+        upk[kk] = jnp.zeros(upk.shape[1:], F32)
 
         def one(step):
             index = pair_at(step)
-            lows = jnp.concatenate([lowbuf[2 * index], lowbuf[2 * index + 1]], axis=1)
-            total[:, :rank] += dot(weight[kk, step], lows, NT) * facs[kk, step][:, :rank]
+            low = jnp.concatenate([lowbuf[2 * index, 0], lowbuf[2 * index + 1, 0]], axis=1)
+            upk[kk] += dot(low, vgrad[kk, step], NN)
 
         each(0, pairs, one)
-        sides = split(total[:, :rank])
-        both = dot(sides, stacked(gs, kk), TN)
-        upk[kk] = both[:rank] + both[rank:]
 
     each(0, KEY_HEADS, low_weights)
+    values.forward(3)
     share = KEY_HEADS // reps
 
     def swap_up(r):
@@ -410,7 +453,7 @@
         return remote(tbuf.at[rep], tbuf.at[rep], t_send.at[r], t_recv.at[rep], own, r)
 
     other_reps(lambda r: swap_total(r).start())
-    loads[4].wait()
+    loads[3].wait()
 
     def arrivals(r):
         remote(
@@ -462,30 +505,34 @@
 
     owners(lambda node: reduce_copy(own, node).start())
 
-    each(0, pair + 1, lambda t: from_partner(vbuf, v_fwd, v_recv, t))
-
     def outputs(kk):
+        each(0, pair + 1, lambda t: values.from_partner(t, kk))
         grad = stacked(gs, kk)
-        total[...] = jnp.zeros_like(total)
+        acc[...] = jnp.zeros_like(acc)
 
         def attend(step):
-            total[...] += dot(weight[kk, step], two(vbuf, pair_at(step), kk), NN) * facs[kk, step]
+            acc[...] += times(
+                dot(two(vbuf, pair_at(step), kk), weight[kk, step], TN), facs[kk, step]
+            )
 
         each(0, pairs, attend)
-        out = total[...]
-        atts[pl.ds(kk * per, per)] = out.astype(BF16).reshape(per, block, HEAD_SIZE)
-        dots = jnp.sum(grad.astype(F32) * out, axis=1, keepdims=True)
-        total[...] = jnp.zeros_like(total)
+        out = acc[...]
+        dots = (gtr[kk].astype(F32) * out).reshape(HEAD_SIZE // 8, 8, rows)
+        dots = eight(jnp.sum(jnp.sum(dots, axis=0), axis=0, keepdims=True))
+        for i in range(per):
+            atts[kk * per + i] = acc[:, i * block:(i + 1) * block].T.astype(BF16)
+        acc[...] = jnp.zeros_like(acc)
 
         def back(step):
             index = pair_at(step)
-            pressure = dot(grad, two(vbuf, index, kk), NT)
-            slope = facs[kk, step] * scale
-            slopes = (score[kk, step] * ((pressure - dots) * jnp.concatenate([slope, slope], axis=1))).astype(BF16)
-            total[...] += dot(slopes, two(kbuf, index, kk), NN)
+            pressure = dot(two(vbuf, index, kk), grad, NT).reshape(eights, 8, rows)
+            slopes = (pressure - dots[None]) * (facs[kk, step] * scale)[None]
+            slopes = score[kk, step] * slopes.reshape(2 * block, rows)
+            acc[...] += dot(two(kbuf, index, kk), slopes.astype(BF16), TN)
 
         each(0, pairs, back)
-        qgs[pl.ds(kk * per, per)] = total[...].astype(BF16).reshape(per, block, HEAD_SIZE)
+        for i in range(per):
+            qgs[kk * per + i] = acc[:, i * block:(i + 1) * block].T.astype(BF16)
 
         def store(i):
             head_store(atts, att_ref, store_a, i).start()
@@ -493,7 +540,7 @@
 
         each(kk * per, (kk + 1) * per, store)
 
-    outputs_early = 1
+    outputs_early = 2
     each(0, outputs_early, outputs)
 
     def gather_copy(node, owner):
@@ -537,9 +584,9 @@
         ).wait_recv())
 
     other_reps(from_reps)
-    drain(kbuf, k_col, k_fwd, k_recv)
-    drain(lowbuf, l_col, l_fwd, l_recv)
-    drain(vbuf, v_col, v_fwd, v_recv)
+    each(0, KEY_HEADS, keys.drain)
+    lows.drain(0)
+    each(0, KEY_HEADS, values.drain)
     other_reps(lambda r: swap_x(r).wait_send())
     ancestors(lambda t: scatter(own, t).wait_send())
     other_reps(lambda r: swap_up(r).wait_send())
@@ -631,21 +678,25 @@
             v(x.shape, BF16), v((reps, block, width // reps), BF16), v((rank, width), BF16),
             v((heads, block, HEAD_SIZE), BF16), v((heads, block, HEAD_SIZE), BF16),
             v(frozen.shape, BF16),
-            v((slots, block, up_width), BF16), v((slots, block, up_width), BF16),
-            v((slots, rank, block), BF16),
-            v((KEY_HEADS, pairs, rows, 2 * block), F32),
-            v((KEY_HEADS, pairs, rows, 2 * block), BF16),
-            v((KEY_HEADS, pairs, rows, HEAD_SIZE), F32), v((KEY_HEADS, pairs, rows, HEAD_SIZE), F32),
-            v((rows, HEAD_SIZE), F32), v((KEY_HEADS, rows, rank), F32),
+            v((slots, KEY_HEADS, block, HEAD_SIZE), BF16),
+            v((slots, KEY_HEADS, block, HEAD_SIZE), BF16),
+            v((slots, 1, rank, block), BF16),
+            v((KEY_HEADS, pairs, 2 * block, rows), F32),
+            v((KEY_HEADS, pairs, 2 * block, rows), BF16),
+            v((KEY_HEADS, pairs, 8, rows), F32), v((KEY_HEADS, pairs, 8, rows), F32),
+            v((HEAD_SIZE, rows), F32), v((KEY_HEADS, rank, rows), F32),
+            v((KEY_HEADS, HEAD_SIZE, rows), BF16),
+            v((KEY_HEADS, pairs, 2 * block, HEAD_SIZE), BF16),
+            v((pairs, 2 * block, 2 * rank), F32),
             v((heads, block, HEAD_SIZE), BF16), v((heads, block, HEAD_SIZE), BF16),
             v((slots, rank, block), F32), v((slots, rank, block), F32),
             v((reps, rank, block), BF16),
             v((KEY_HEADS, rank, HEAD_SIZE), F32), v((reps, share, rank, HEAD_SIZE), F32),
             v((chunks, rank, chunk), BF16), v((slots, rank, chunk), BF16),
-            dma((5,)), dma((heads,)), dma((heads,)), dma((heads,)), dma((heads,)),
-            dma((slots,)), dma((slots,)), dma((slots,)),
-            dma((slots,)), dma((slots,)), dma((slots,)),
-            dma((slots,)), dma((slots,)), dma((slots,)),
+            dma((4,)), dma((KEY_HEADS,)), dma((heads,)), dma((heads,)), dma((heads,)), dma((heads,)),
+            dma((slots, KEY_HEADS)), dma((slots, KEY_HEADS)), dma((slots, KEY_HEADS)),
+            dma((slots, 1)), dma((slots, 1)), dma((slots, 1)),
+            dma((slots, KEY_HEADS)), dma((slots, KEY_HEADS)), dma((slots, KEY_HEADS)),
             dma((reps,)), dma((reps,)), dma((slots,)), dma((slots,)),
             dma((reps,)), dma((reps,)), dma((reps,)), dma((reps,)),
             dma((slots,)), dma((slots,)), dma((slots,)), dma((slots,)),

time: 68.6 us -> 60.5 us (0.88)
  Pallas kernels: 67.4 us -> 59.1 us
    pallas_call x1, Pallas kernels: 64.6 us -> 56.4 us  [on_device(): pl.pallas_call(functools.partial(kernel, slots, reps, factor), in_specs=[...]
where the time goes in v3:
time: 60.5 us; the launch traced here: 59.7 us
  Pallas kernels  59.1 us (98%)
  between operations  0.64 us (1%)
    pallas_call x1, Pallas kernels, on_device(): pl.pallas_call(functools.partial(kernel, slots, reps, factor), in_specs=[...  56.4 us
    pallas_call x1, Pallas kernels, on_device(): pl.pallas_call(functools.partial(finish, cuts), in_specs=[anywhere, anywh...  2.72 us

profile of v3, /device:TPU:0, one launch (start us, length us, event | category | flops | bytes accessed | tf_op | source)
XLA Modules:
  0.0 59.7 jit_solution(4193600633088353412)
XLA Ops:
  0.6 56.4 %tree_attention.1 = (bf16[128,2560]{1,0:T(8,128)(2,1)}, bf16[128,2560]{1,0:T(8,128)(2,1)}, bf16[2,8,32,384]{3,2,1,0:T(8,128)(2,1)}) custom-call(s32[1,8]{1,0:T(1,128)} %parents.1, s32[1,8]{1,0:T(1,128)} %lengths.1, bf16[128,5120]{1,0:T(8,128)(2,1)} %bitcast.9, bf16[128,2560]{1,0:T(8,128)(2,1)} %bitcast.10, bf16[128,512]{1,0:T(8,128)(2,1)} %bitcast.13, ...), custom_call_target="tpu_custom_call" | custom-call | tf_op jit(solution)/shard_map/tree_attention/pallas_call | solution.py:668
  57.0 2.7 %finish.1 = (bf16[128,2560]{1,0:T(8,128)(2,1)}, bf16[128,2560]{1,0:T(8,128)(2,1)}, f32[32,5120]{1,0:T(8,128)}, f32[32,512]{1,0:T(8,128)}) custom-call(bf16[128,2560]{1,0:T(8,128)(2,1)} %get-tuple-element.11.a_ref, bf16[128,2560]{1,0:T(8,128)(2,1)} %get-tuple-element.12.b_ref, bf16[2,8,32,384]{3,2,1,0:T(8,128)(2,1)} %get-tuple-element.13.r_ref), custom_call_target="tpu_custom_call" | custom-call | tf_op jit(solution)/shard_map/finish/pallas_call | solution.py:711

commit v4 on v3

--- a/solution.py
+++ b/solution.py
@@ -53,11 +53,10 @@
     parents, lengths, x_ref, q_ref, k_ref, frozen_ref, down_ref, up_ref, g_ref,
     att_ref, qg_ref, result,
     xs, xcat, downs, qs, gs, fs, kbuf, vbuf, lowbuf, score, weight, tops, facs, acc, gup, gtr,
-    vgrad, both, atts, qgs, proj, landed, tbuf, upk, upland, parts, gathered,
-    load_sem, kload, qload, gload, store_a, store_q,
-    k_col, k_fwd, k_recv, l_col, l_fwd, l_recv, v_col, v_fwd, v_recv,
-    x_send, x_recv, p_send, p_recv, t_send, t_recv, u_send, u_recv,
-    r_send, r_recv, a_send, a_recv, b_send, b_recv,
+    vgrad, both, invs, atts, qgs, proj, mine, landed, tbuf, upk, upland, parts, gathered,
+    load_sem, stored, k_recv, l_recv, v_recv, col_send, fwd_send, l_col, l_fwd,
+    x_recv, x_send, t_recv, t_send, u_recv, u_send, p_recv, p_send,
+    r_recv, r_send, a_recv, a_send, b_recv, b_send,
 ):
     own, rep = lax.axis_index("node"), lax.axis_index("rep")
     heads = qs.shape[0]
@@ -101,7 +100,7 @@
     def key_load(kk):
         return pltpu.make_async_copy(
             k_ref.at[:, pl.ds(pl.multiple_of(kk * HEAD_SIZE, HEAD_SIZE), HEAD_SIZE)],
-            kbuf.at[own, kk], kload.at[kk],
+            kbuf.at[own, kk], load_sem.at[4],
         )
 
     for kk in range(KEY_HEADS):
@@ -112,15 +111,18 @@
     def head_copy(source, target, sem, i):
         return pltpu.make_async_copy(
             source.at[:, pl.ds(pl.multiple_of(i * HEAD_SIZE, HEAD_SIZE), HEAD_SIZE)],
-            target.at[i], sem.at[i],
+            target.at[i], sem,
         )
 
     def head_store(source, target, sem, i):
         return pltpu.make_async_copy(
             source.at[i],
             target.at[:, pl.ds(pl.multiple_of(i * HEAD_SIZE, HEAD_SIZE), HEAD_SIZE)],
-            sem.at[i],
-        )
+            sem,
+        )
+
+    def all_of(buf, sem):
+        return pltpu.make_async_copy(buf, buf, sem)
 
     def each(low, high, action):
         def body(i, carry):
@@ -129,8 +131,8 @@
 
         lax.fori_loop(low, high, body, 0)
 
-    each(0, heads, lambda i: head_copy(q_ref, qs, qload, i).start())
-    each(0, heads, lambda i: head_copy(g_ref, gs, gload, i).start())
+    each(0, heads, lambda i: head_copy(q_ref, qs, load_sem.at[5], i).start())
+    each(0, heads, lambda i: head_copy(g_ref, gs, load_sem.at[6], i).start())
 
     chain = []
     current = own
@@ -152,8 +154,6 @@
         return jnp.logical_not(lands | (slot == own))
 
     def clear_slot(slot):
-        proj[slot] = jnp.zeros(proj.shape[1:], F32)
-
         @pl.when(unsent(slot))
         def _():
             kbuf[slot] = jnp.zeros(kbuf.shape[1:], BF16)
@@ -162,8 +162,7 @@
 
     each(0, slots, clear_slot)
 
-    for kk in range(KEY_HEADS):
-        key_load(kk).wait()
+    all_of(kbuf.at[own], load_sem.at[4]).wait()
     pl.semaphore_wait(barrier, slots * reps - 1)
 
     class Stream:
@@ -171,33 +170,37 @@
             self.buf, self.col, self.fwd, self.recv = buf, col, fwd, recv
 
         def column(self, t, kk):
+            block = self.buf.at[own, kk]
+            return remote(block, block, self.col.at[t], self.recv(own, kk), own + 2 * t)
+
+        def across(self, slot, kk):
+            block = self.buf.at[slot, kk]
             return remote(
-                self.buf.at[own, kk], self.buf.at[own, kk], self.col.at[t, kk],
-                self.recv.at[own, kk], own + 2 * t,
+                block, block, self.fwd.at[(own - slot) // 2], self.recv(slot, kk), partner
             )
 
-        def across(self, slot, kk):
-            return remote(
-                self.buf.at[slot, kk], self.buf.at[slot, kk], self.fwd.at[slot, kk],
-                self.recv.at[slot, kk], partner,
-            )
-
-        def own_copies(self, kk, action):
+        def arrival(self, slot, kk):
+            block = self.buf.at[slot, kk]
+            return remote(block, block, self.fwd.at[0], self.recv(slot, kk), partner)
+
+        def targets(self, across, column):
             @pl.when(reaches(own, partner))
             def _():
-                action(self.across(own, kk))
+                across()
 
             def body(step):
                 t = slots // 2 - 1 - step
 
                 @pl.when((own + 2 * t < slots) & reaches(own, 2 * (pair + t)))
                 def _():
-                    action(self.column(t, kk))
+                    column(t)
 
             each(0, slots // 2 - 1, body)
 
         def send(self, kk):
-            self.own_copies(kk, lambda c: c.start())
+            self.targets(
+                lambda: self.across(own, kk).start(), lambda t: self.column(t, kk).start()
+            )
 
         def forward(self, kk):
             def body(t):
@@ -205,7 +208,7 @@
 
                 @pl.when(reaches(slot, 2 * pair))
                 def _():
-                    self.across(slot, kk).wait_recv()
+                    self.arrival(slot, kk).wait_recv()
 
                     @pl.when(reaches(slot, partner))
                     def _():
@@ -218,23 +221,26 @@
 
             @pl.when(reaches(slot, own))
             def _():
-                self.across(slot, kk).wait_recv()
-
-        def drain(self, kk):
-            self.own_copies(kk, lambda c: c.wait_send())
+                self.arrival(slot, kk).wait_recv()
+
+        def drain(self, sent):
+            self.targets(
+                lambda: all_of(sent, self.fwd.at[0]).wait(),
+                lambda t: all_of(sent, self.col.at[t]).wait(),
+            )
 
             def body(t):
                 slot = own - 2 * t
 
                 @pl.when(reaches(slot, 2 * pair) & reaches(slot, partner))
                 def _():
-                    self.across(slot, kk).wait_send()
+                    all_of(sent, self.fwd.at[t]).wait()
 
             each(1, pair + 1, body)
 
-    keys = Stream(kbuf, k_col, k_fwd, k_recv)
-    values = Stream(vbuf, v_col, v_fwd, v_recv)
-    lows = Stream(lowbuf, l_col, l_fwd, l_recv)
+    keys = Stream(kbuf, col_send, fwd_send, lambda slot, kk: k_recv.at[slot, kk])
+    values = Stream(vbuf, col_send, fwd_send, lambda slot, kk: v_recv.at[slot, kk])
+    lows = Stream(lowbuf, l_col, l_fwd, lambda slot, kk: l_recv.at[slot])
     each(0, KEY_HEADS, keys.send)
 
     def swap_x(r):
@@ -259,8 +265,8 @@
         vbuf[own, kk] = own_values[:, kk * HEAD_SIZE:(kk + 1) * HEAD_SIZE]
     lows.send(0)
 
-    each(0, heads, lambda i: head_copy(q_ref, qs, qload, i).wait())
-    each(0, heads, lambda i: head_copy(g_ref, gs, gload, i).wait())
+    all_of(qs, load_sem.at[5]).wait()
+    all_of(gs, load_sem.at[6]).wait()
 
     def stacked(buf, kk):
         return buf[pl.ds(kk * per, per)].reshape(rows, HEAD_SIZE)
@@ -336,6 +342,10 @@
         def _():
             keys.forward(kk + 1)
 
+        @pl.when(kk == KEY_HEADS - 1)
+        def _():
+            lows.forward(0)
+
         own_pair(kk)
 
         @pl.when(kk == 0)
@@ -350,11 +360,6 @@
         lax.rem(lax.broadcasted_iota(jnp.int32, (8, rows), 1), block) < own_length
     ).astype(F32)
 
-    def clear_both(step):
-        both[step] = jnp.zeros(both.shape[1:], F32)
-
-    each(0, pairs, clear_both)
-
     def weigh(kk):
         most = tops[kk, pairs - 1]
 
@@ -364,10 +369,22 @@
             facs[kk, step] = fall
             return total
 
-        inverse = live / lax.fori_loop(0, pairs, add, jnp.zeros((8, rows), F32))
-
-        def project(step):
-            fac = facs[kk, step] * inverse
+        invs[kk] = live / lax.fori_loop(0, pairs, add, jnp.zeros((8, rows), F32))
+
+    each(0, KEY_HEADS, weigh)
+
+    def scatter(source, target):
+        return remote(
+            proj.at[target], landed.at[source], p_send.at[target], p_recv.at[source], target
+        )
+
+    def project(i):
+        step = pairs - 1 - i
+        index = pair_at(step)
+        both[...] = jnp.zeros_like(both)
+
+        def head(kk):
+            fac = facs[kk, step] * invs[kk]
             facs[kk, step] = fac
             side = times(gup[kk], fac)
             high = side.astype(BF16)
@@ -377,25 +394,21 @@
             )
             out = dot(weight[kk, step], right, NT)
             vgrad[kk, step] = out[:, :HEAD_SIZE].astype(BF16)
-            both[step] += out[:, HEAD_SIZE:]
-
-        each(0, pairs, project)
-
-    each(0, KEY_HEADS, weigh)
-
-    def place(step):
-        index = pair_at(step)
-        turned = both[step].T
+            both[...] += out[:, HEAD_SIZE:]
+
+        each(0, KEY_HEADS, head)
+        turned = both[...].T
         turned = turned[:rank] + turned[rank:]
-        proj[2 * index] = turned[:, :block]
-        proj[2 * index + 1] = turned[:, block:]
-
-    each(0, pairs, place)
-
-    def scatter(source, target):
-        return remote(
-            proj.at[target], landed.at[source], p_send.at[target], p_recv.at[source], target
-        )
+        for parity in range(2):
+            slot = 2 * index + parity
+            mine[parity] = turned[:, parity * block:(parity + 1) * block]
+            proj[slot] = mine[parity].astype(BF16)
+
+            @pl.when(reaches(slot, own))
+            def _():
+                scatter(own, slot).start()
+
+    each(0, pairs, project)
 
     def ancestors(action):
         def body(t):
@@ -413,8 +426,6 @@
 
         each(0, slots, body)
 
-    ancestors(lambda t: scatter(own, t).start())
-    lows.forward(0)
     values.forward(1)
     values.forward(2)
     each(0, pair + 1, lambda t: lows.from_partner(t, 0))
@@ -440,14 +451,19 @@
 
     other_reps(lambda r: swap_up(r).start())
 
+    descendants(lambda t: remote(
+        proj.at[t], landed.at[t], p_send.at[t], p_recv.at[t], t
+    ).wait_recv())
+    total = mine[lax.rem(own, 2)]
+
     def add_landed(t):
-        remote(
-            proj.at[t], landed.at[t], p_send.at[t], p_recv.at[t], t
-        ).wait_recv()
-        proj[own] += landed[t]
-
-    descendants(add_landed)
-    tbuf[rep] = proj[own].astype(BF16)
+        @pl.when(reaches(own, t))
+        def _():
+            mine[0] += landed[t].astype(F32)
+
+    mine[0] = total
+    each(0, slots, add_landed)
+    tbuf[rep] = mine[0].astype(BF16)
 
     def swap_total(r):
         return remote(tbuf.at[rep], tbuf.at[rep], t_send.at[r], t_recv.at[rep], own, r)
@@ -489,7 +505,7 @@
 
     def reduce_copy(source, node):
         return remote(
-            parts.at[node], gathered.at[source], r_send.at[node], r_recv.at[source], node
+            parts.at[node], gathered.at[source], r_send, r_recv, node
         )
 
     def others(action):
@@ -535,8 +551,8 @@
             qgs[kk * per + i] = acc[:, i * block:(i + 1) * block].T.astype(BF16)
 
         def store(i):
-            head_store(atts, att_ref, store_a, i).start()
-            head_store(qgs, qg_ref, store_q, i).start()
+            head_store(atts, att_ref, stored.at[0], i).start()
+            head_store(qgs, qg_ref, stored.at[1], i).start()
 
         each(kk * per, (kk + 1) * per, store)
 
@@ -545,21 +561,18 @@
 
     def gather_copy(node, owner):
         return remote(
-            result.at[rep, owner], result.at[rep, owner], a_send.at[node], a_recv.at[owner], node
+            result.at[rep, owner], result.at[rep, owner], a_send, a_recv.at[owner], node
         )
 
     def swap_result(r, owner):
         return remote(
-            result.at[rep, owner], result.at[rep, owner], b_send.at[r, owner],
-            b_recv.at[rep, owner], own, r,
+            result.at[rep, owner], result.at[rep, owner], b_send.at[r], b_recv.at[rep], own, r
         )
 
     @pl.when(own < chunks)
     def _():
         gathered[own] = parts[own]
-        others(lambda node: remote(
-            parts.at[own], gathered.at[node], r_send.at[node], r_recv.at[node], node
-        ).wait_recv())
+        all_of(gathered.at[pl.ds(0, slots - 1)], r_recv).wait()
         acc = lax.fori_loop(
             0, slots, lambda t, a: a + gathered[t].astype(F32), jnp.zeros((rank, chunk), F32)
         )
@@ -571,35 +584,32 @@
 
     def pass_on(owner):
         remote(
-            result.at[rep, owner], result.at[rep, owner], a_send.at[owner], a_recv.at[owner], owner
+            result.at[rep, owner], result.at[rep, owner], a_send, a_recv.at[owner], owner
         ).wait_recv()
         other_reps(lambda r: swap_result(r, owner).start())
 
     owners(pass_on)
 
-    def from_reps(r):
-        each(0, chunks, lambda owner: remote(
-            result.at[r, owner], result.at[r, owner], b_send.at[r, owner], b_recv.at[r, owner],
-            own, r,
-        ).wait_recv())
-
-    other_reps(from_reps)
-    each(0, KEY_HEADS, keys.drain)
-    lows.drain(0)
-    each(0, KEY_HEADS, values.drain)
+    other_reps(lambda r: all_of(result.at[r], b_recv.at[r]).wait())
+    keys.drain(kbuf.at[pl.ds(0, 2)])
+    lows.drain(lowbuf.at[0])
     other_reps(lambda r: swap_x(r).wait_send())
     ancestors(lambda t: scatter(own, t).wait_send())
     other_reps(lambda r: swap_up(r).wait_send())
     other_reps(lambda r: swap_total(r).wait_send())
-    owners(lambda node: reduce_copy(own, node).wait_send())
 
     @pl.when(own < chunks)
     def _():
-        others(lambda node: gather_copy(node, own).wait_send())
-
-    other_reps(lambda r: each(0, chunks, lambda owner: swap_result(r, owner).wait_send()))
-    each(0, heads, lambda i: head_store(atts, att_ref, store_a, i).wait())
-    each(0, heads, lambda i: head_store(qgs, qg_ref, store_q, i).wait())
+        all_of(parts.at[pl.ds(0, chunks - 1)], r_send).wait()
+        all_of(gathered.at[pl.ds(0, slots - 1)], a_send).wait()
+
+    @pl.when(own >= chunks)
+    def _():
+        all_of(parts, r_send).wait()
+
+    other_reps(lambda r: all_of(result.at[rep], b_send.at[r]).wait())
+    all_of(atts, stored.at[0]).wait()
+    all_of(qgs, stored.at[1]).wait()
 
 
 def finish(cuts, a_ref, b_ref, r_ref, att_ref, qg_ref, down_ref, up_ref, a, b, res, down, up, ins, outs, sems):
@@ -687,20 +697,17 @@
             v((HEAD_SIZE, rows), F32), v((KEY_HEADS, rank, rows), F32),
             v((KEY_HEADS, HEAD_SIZE, rows), BF16),
             v((KEY_HEADS, pairs, 2 * block, HEAD_SIZE), BF16),
-            v((pairs, 2 * block, 2 * rank), F32),
+            v((2 * block, 2 * rank), F32), v((KEY_HEADS, 8, rows), F32),
             v((heads, block, HEAD_SIZE), BF16), v((heads, block, HEAD_SIZE), BF16),
-            v((slots, rank, block), F32), v((slots, rank, block), F32),
+            v((slots, rank, block), BF16), v((2, rank, block), F32), v((slots, rank, block), BF16),
             v((reps, rank, block), BF16),
             v((KEY_HEADS, rank, HEAD_SIZE), F32), v((reps, share, rank, HEAD_SIZE), F32),
             v((chunks, rank, chunk), BF16), v((slots, rank, chunk), BF16),
-            dma((4,)), dma((KEY_HEADS,)), dma((heads,)), dma((heads,)), dma((heads,)), dma((heads,)),
-            dma((slots, KEY_HEADS)), dma((slots, KEY_HEADS)), dma((slots, KEY_HEADS)),
-            dma((slots, 1)), dma((slots, 1)), dma((slots, 1)),
-            dma((slots, KEY_HEADS)), dma((slots, KEY_HEADS)), dma((slots, KEY_HEADS)),
-            dma((reps,)), dma((reps,)), dma((slots,)), dma((slots,)),
-            dma((reps,)), dma((reps,)), dma((reps,)), dma((reps,)),
-            dma((slots,)), dma((slots,)), dma((slots,)), dma((slots,)),
-            dma((reps, chunks)), dma((reps, chunks)),
+            dma((7,)), dma((2,)),
+            dma((slots, KEY_HEADS)), dma((slots,)), dma((slots, KEY_HEADS)),
+            dma((slots // 2,)), dma((slots // 2,)), dma((slots // 2,)), dma((slots // 2,)),
+            dma((reps,)), dma((reps,)), dma((reps,)), dma((reps,)), dma((reps,)), dma((reps,)),
+            dma((slots,)), dma((slots,)), dma, dma, dma((slots,)), dma, dma((reps,)), dma((reps,)),
         ],
         compiler_params=pltpu.CompilerParams(
             collective_id=0, has_side_effects=True, vmem_limit_bytes=60 * 1024 * 1024

time: 60.5 us -> 55 us (0.909)
  Pallas kernels: 59.1 us -> 54.2 us
    pallas_call x1, Pallas kernels: 56.4 us -> 51.4 us  [on_device(): pl.pallas_call(functools.partial(kernel, slots, reps, factor), in_specs=[...]
where the time goes in v4:
time: 55 us; the launch traced here: 54.8 us
  Pallas kernels  54.2 us (99%)
  between operations  0.64 us (1%)
    pallas_call x1, Pallas kernels, on_device(): pl.pallas_call(functools.partial(kernel, slots, reps, factor), in_specs=[...  51.4 us
    pallas_call x1, Pallas kernels, on_device(): pl.pallas_call(functools.partial(finish, cuts), in_specs=[anywhere, anywh...  2.72 us

profile of v4, /device:TPU:0, one launch (start us, length us, event | category | flops | bytes accessed | tf_op | source)
XLA Modules:
  0.0 54.8 jit_solution(7161405506565067927)
XLA Ops:
  0.6 51.4 %tree_attention.1 = (bf16[128,2560]{1,0:T(8,128)(2,1)}, bf16[128,2560]{1,0:T(8,128)(2,1)}, bf16[2,8,32,384]{3,2,1,0:T(8,128)(2,1)}) custom-call(s32[1,8]{1,0:T(1,128)} %parents.1, s32[1,8]{1,0:T(1,128)} %lengths.1, bf16[128,5120]{1,0:T(8,128)(2,1)} %bitcast.9, bf16[128,2560]{1,0:T(8,128)(2,1)} %bitcast.10, bf16[128,512]{1,0:T(8,128)(2,1)} %bitcast.13, ...), custom_call_target="tpu_custom_call" | custom-call | tf_op jit(solution)/shard_map/tree_attention/pallas_call | solution.py:678
  52.1 2.7 %finish.1 = (bf16[128,2560]{1,0:T(8,128)(2,1)}, bf16[128,2560]{1,0:T(8,128)(2,1)}, f32[32,5120]{1,0:T(8,128)}, f32[32,512]{1,0:T(8,128)}) custom-call(bf16[128,2560]{1,0:T(8,128)(2,1)} %get-tuple-element.11.a_ref, bf16[128,2560]{1,0:T(8,128)(2,1)} %get-tuple-element.12.b_ref, bf16[2,8,32,384]{3,2,1,0:T(8,128)(2,1)} %get-tuple-element.13.r_ref), custom_call_target="tpu_custom_call" | custom-call | tf_op jit(solution)/shard_map/finish/pallas_call | solution.py:718

commit v5 on v4

--- a/solution.py
+++ b/solution.py
@@ -54,7 +54,7 @@
     att_ref, qg_ref, result,
     xs, xcat, downs, qs, gs, fs, kbuf, vbuf, lowbuf, score, weight, tops, facs, acc, gup, gtr,
     vgrad, both, invs, atts, qgs, proj, mine, landed, tbuf, upk, upland, parts, gathered,
-    load_sem, stored, k_recv, l_recv, v_recv, col_send, fwd_send, l_col, l_fwd,
+    load_sem, stored, k_recv, l_recv, v_recv, col_send, fwd_send, on_send, turn_send, l_col, l_fwd, l_on,
     x_recv, x_send, t_recv, t_send, u_recv, u_send, p_recv, p_send,
     r_recv, r_send, a_recv, a_send, b_recv, b_send,
 ):
@@ -166,81 +166,85 @@
     pl.semaphore_wait(barrier, slots * reps - 1)
 
     class Stream:
-        def __init__(self, buf, col, fwd, recv):
-            self.buf, self.col, self.fwd, self.recv = buf, col, fwd, recv
-
-        def column(self, t, kk):
-            block = self.buf.at[own, kk]
-            return remote(block, block, self.col.at[t], self.recv(own, kk), own + 2 * t)
-
-        def across(self, slot, kk):
+        def __init__(self, buf, col, fwd, on, recv, turns=False):
+            self.buf, self.col, self.fwd, self.on, self.recv = buf, col, fwd, on, recv
+            self.turns = turns
+
+        def move(self, slot, kk, send, node):
             block = self.buf.at[slot, kk]
-            return remote(
-                block, block, self.fwd.at[(own - slot) // 2], self.recv(slot, kk), partner
-            )
-
-        def arrival(self, slot, kk):
-            block = self.buf.at[slot, kk]
-            return remote(block, block, self.fwd.at[0], self.recv(slot, kk), partner)
+            return remote(block, block, send, self.recv(slot, kk), node)
+
+        def arrived(self, slot, kk):
+            self.move(slot, kk, self.fwd.at[0], partner).wait_recv()
 
         def targets(self, across, column):
             @pl.when(reaches(own, partner))
             def _():
                 across()
 
-            def body(step):
-                t = slots // 2 - 1 - step
-
+            for t in (2, 1):
                 @pl.when((own + 2 * t < slots) & reaches(own, 2 * (pair + t)))
                 def _():
                     column(t)
 
-            each(0, slots // 2 - 1, body)
-
         def send(self, kk):
             self.targets(
-                lambda: self.across(own, kk).start(), lambda t: self.column(t, kk).start()
+                lambda: self.move(own, kk, self.fwd.at[0], partner).start(),
+                lambda t: self.move(own, kk, self.col.at[t], own + 2 * t).start(),
             )
 
-        def forward(self, kk):
+        def passing(self, receive, onward, across):
             def body(t):
                 slot = own - 2 * t
 
                 @pl.when(reaches(slot, 2 * pair))
                 def _():
-                    self.arrival(slot, kk).wait_recv()
-
-                    @pl.when(reaches(slot, partner))
+                    receive(slot)
+
+                    @pl.when((t >= 2) & (own + 2 < slots) & reaches(slot, 2 * pair + 2))
                     def _():
-                        self.across(slot, kk).start()
+                        onward(slot, t)
+
+                    crosses = reaches(slot, partner)
+                    if self.turns:
+                        crosses = crosses & ((t > 1) | (own > partner))
+
+                    @pl.when(crosses)
+                    def _():
+                        across(slot, t)
 
             each(1, pair + 1, body)
+
+        def turning(self, action):
+            @pl.when((own > partner) & (own + 2 < slots) & reaches(partner, own + 2))
+            def _():
+                action()
+
+        def forward(self, kk):
+            if self.turns:
+                @pl.when(own > partner)
+                def _():
+                    self.arrived(partner, kk)
+
+                self.turning(lambda: self.move(partner, kk, turn_send, own + 2).start())
+            self.passing(
+                lambda slot: self.arrived(slot, kk),
+                lambda slot, t: self.move(slot, kk, self.on.at[t], own + 2).start(),
+                lambda slot, t: self.move(slot, kk, self.fwd.at[t], partner).start(),
+            )
 
         def from_partner(self, t, kk):
             slot = partner - 2 * t
 
-            @pl.when(reaches(slot, own))
+            @pl.when(reaches(slot, own) & ((t > 0) | (not self.turns)))
             def _():
-                self.arrival(slot, kk).wait_recv()
-
-        def drain(self, sent):
-            self.targets(
-                lambda: all_of(sent, self.fwd.at[0]).wait(),
-                lambda t: all_of(sent, self.col.at[t]).wait(),
-            )
-
-            def body(t):
-                slot = own - 2 * t
-
-                @pl.when(reaches(slot, 2 * pair) & reaches(slot, partner))
-                def _():
-                    all_of(sent, self.fwd.at[t]).wait()
-
-            each(1, pair + 1, body)
-
-    keys = Stream(kbuf, col_send, fwd_send, lambda slot, kk: k_recv.at[slot, kk])
-    values = Stream(vbuf, col_send, fwd_send, lambda slot, kk: v_recv.at[slot, kk])
-    lows = Stream(lowbuf, l_col, l_fwd, lambda slot, kk: l_recv.at[slot])
+                self.arrived(slot, kk)
+
+    keys = Stream(kbuf, col_send, fwd_send, on_send, lambda slot, kk: k_recv.at[slot, kk])
+    values = Stream(
+        vbuf, col_send, fwd_send, on_send, lambda slot, kk: v_recv.at[slot, kk], turns=True
+    )
+    lows = Stream(lowbuf, l_col, l_fwd, l_on, lambda slot, kk: l_recv.at[slot])
     each(0, KEY_HEADS, keys.send)
 
     def swap_x(r):
@@ -591,8 +595,38 @@
     owners(pass_on)
 
     other_reps(lambda r: all_of(result.at[r], b_recv.at[r]).wait())
-    keys.drain(kbuf.at[pl.ds(0, 2)])
-    lows.drain(lowbuf.at[0])
+    heads_of_two = kbuf.at[pl.ds(0, 2)]
+
+    def crossed(t):
+        both_cross = (t > 1) | (own > partner)
+
+        @pl.when(both_cross)
+        def _():
+            all_of(heads_of_two, fwd_send.at[t]).wait()
+
+        @pl.when(jnp.logical_not(both_cross))
+        def _():
+            all_of(kbuf.at[0], fwd_send.at[t]).wait()
+
+    keys.targets(
+        lambda: all_of(heads_of_two, fwd_send.at[0]).wait(),
+        lambda t: all_of(heads_of_two, col_send.at[t]).wait(),
+    )
+    keys.passing(
+        lambda slot: None,
+        lambda slot, t: all_of(heads_of_two, on_send.at[t]).wait(),
+        lambda slot, t: crossed(t),
+    )
+    values.turning(lambda: all_of(kbuf.at[0], turn_send).wait())
+    lows.targets(
+        lambda: all_of(lowbuf.at[0], l_fwd.at[0]).wait(),
+        lambda t: all_of(lowbuf.at[0], l_col.at[t]).wait(),
+    )
+    lows.passing(
+        lambda slot: None,
+        lambda slot, t: all_of(lowbuf.at[0], l_on.at[t]).wait(),
+        lambda slot, t: all_of(lowbuf.at[0], l_fwd.at[t]).wait(),
+    )
     other_reps(lambda r: swap_x(r).wait_send())
     ancestors(lambda t: scatter(own, t).wait_send())
     other_reps(lambda r: swap_up(r).wait_send())
@@ -705,7 +739,8 @@
             v((chunks, rank, chunk), BF16), v((slots, rank, chunk), BF16),
             dma((7,)), dma((2,)),
             dma((slots, KEY_HEADS)), dma((slots,)), dma((slots, KEY_HEADS)),
-            dma((slots // 2,)), dma((slots // 2,)), dma((slots // 2,)), dma((slots // 2,)),
+            dma((3,)), dma((slots // 2,)), dma((slots // 2,)), dma,
+            dma((3,)), dma((slots // 2,)), dma((slots // 2,)),
             dma((reps,)), dma((reps,)), dma((reps,)), dma((reps,)), dma((reps,)), dma((reps,)),
             dma((slots,)), dma((slots,)), dma, dma, dma((slots,)), dma, dma((reps,)), dma((reps,)),
         ],

time: 55 us -> 53.4 us (0.971)
  Pallas kernels: 54.2 us -> 52.5 us
    pallas_call x1, Pallas kernels: 51.4 us -> 49.8 us  [on_device(): pl.pallas_call(functools.partial(kernel, slots, reps, factor), in_specs=[...]
where the time goes in v5:
time: 53.4 us; the launch traced here: 53.2 us
  Pallas kernels  52.5 us (98%)
  between operations  0.64 us (1%)
    pallas_call x1, Pallas kernels, on_device(): pl.pallas_call(functools.partial(kernel, slots, reps, factor), in_specs=[...  49.8 us
    pallas_call x1, Pallas kernels, on_device(): pl.pallas_call(functools.partial(finish, cuts), in_specs=[anywhere, anywh...  2.72 us

profile of v5, /device:TPU:0, one launch (start us, length us, event | category | flops | bytes accessed | tf_op | source)
XLA Modules:
  0.0 53.2 jit_solution(16248933225874578566)
XLA Ops:
  0.6 49.8 %tree_attention.1 = (bf16[128,2560]{1,0:T(8,128)(2,1)}, bf16[128,2560]{1,0:T(8,128)(2,1)}, bf16[2,8,32,384]{3,2,1,0:T(8,128)(2,1)}) custom-call(s32[1,8]{1,0:T(1,128)} %parents.1, s32[1,8]{1,0:T(1,128)} %lengths.1, bf16[128,5120]{1,0:T(8,128)(2,1)} %bitcast.9, bf16[128,2560]{1,0:T(8,128)(2,1)} %bitcast.10, bf16[128,512]{1,0:T(8,128)(2,1)} %bitcast.13, ...), custom_call_target="tpu_custom_call" | custom-call | tf_op jit(solution)/shard_map/tree_attention/pallas_call | solution.py:712
  50.5 2.7 %finish.1 = (bf16[128,2560]{1,0:T(8,128)(2,1)}, bf16[128,2560]{1,0:T(8,128)(2,1)}, f32[32,5120]{1,0:T(8,128)}, f32[32,512]{1,0:T(8,128)}) custom-call(bf16[128,2560]{1,0:T(8,128)(2,1)} %get-tuple-element.11.a_ref, bf16[128,2560]{1,0:T(8,128)(2,1)} %get-tuple-element.12.b_ref, bf16[2,8,32,384]{3,2,1,0:T(8,128)(2,1)} %get-tuple-element.13.r_ref), custom_call_target="tpu_custom_call" | custom-call | tf_op jit(solution)/shard_map/finish/pallas_call | solution.py:753

commit v6 on v5

--- a/solution.py
+++ b/solution.py
@@ -53,8 +53,8 @@
     parents, lengths, x_ref, q_ref, k_ref, frozen_ref, down_ref, up_ref, g_ref,
     att_ref, qg_ref, result,
     xs, xcat, downs, qs, gs, fs, kbuf, vbuf, lowbuf, score, weight, tops, facs, acc, gup, gtr,
-    vgrad, both, invs, atts, qgs, proj, mine, landed, tbuf, upk, upland, parts, gathered,
-    load_sem, stored, k_recv, l_recv, v_recv, col_send, fwd_send, on_send, turn_send, l_col, l_fwd, l_on,
+    vgrad, both, invs, proj, mine, landed, tbuf, upk, upland, parts, gathered,
+    load_sem, k_recv, l_recv, v_recv, col_send, fwd_send, on_send, turn_send, l_col, l_fwd, l_on,
     x_recv, x_send, t_recv, t_send, u_recv, u_send, p_recv, p_send,
     r_recv, r_send, a_recv, a_send, b_recv, b_send,
 ):
@@ -112,13 +112,6 @@
         return pltpu.make_async_copy(
             source.at[:, pl.ds(pl.multiple_of(i * HEAD_SIZE, HEAD_SIZE), HEAD_SIZE)],
             target.at[i], sem,
-        )
-
-    def head_store(source, target, sem, i):
-        return pltpu.make_async_copy(
-            source.at[i],
-            target.at[:, pl.ds(pl.multiple_of(i * HEAD_SIZE, HEAD_SIZE), HEAD_SIZE)],
-            sem,
         )
 
     def all_of(buf, sem):
@@ -540,7 +533,9 @@
         dots = (gtr[kk].astype(F32) * out).reshape(HEAD_SIZE // 8, 8, rows)
         dots = eight(jnp.sum(jnp.sum(dots, axis=0), axis=0, keepdims=True))
         for i in range(per):
-            atts[kk * per + i] = acc[:, i * block:(i + 1) * block].T.astype(BF16)
+            att_ref[:, pl.ds(pl.multiple_of((kk * per + i) * HEAD_SIZE, HEAD_SIZE), HEAD_SIZE)] = (
+                acc[:, i * block:(i + 1) * block].T.astype(BF16)
+            )
         acc[...] = jnp.zeros_like(acc)
 
         def back(step):
@@ -552,13 +547,9 @@
 
         each(0, pairs, back)
         for i in range(per):
-            qgs[kk * per + i] = acc[:, i * block:(i + 1) * block].T.astype(BF16)
-
-        def store(i):
-            head_store(atts, att_ref, stored.at[0], i).start()
-            head_store(qgs, qg_ref, stored.at[1], i).start()
-
-        each(kk * per, (kk + 1) * per, store)
+            qg_ref[:, pl.ds(pl.multiple_of((kk * per + i) * HEAD_SIZE, HEAD_SIZE), HEAD_SIZE)] = (
+                acc[:, i * block:(i + 1) * block].T.astype(BF16)
+            )
 
     outputs_early = 2
     each(0, outputs_early, outputs)
@@ -642,24 +633,17 @@
         all_of(parts, r_send).wait()
 
     other_reps(lambda r: all_of(result.at[rep], b_send.at[r]).wait())
-    all_of(atts, stored.at[0]).wait()
-    all_of(qgs, stored.at[1]).wait()
-
-
-def finish(cuts, a_ref, b_ref, r_ref, att_ref, qg_ref, down_ref, up_ref, a, b, res, down, up, ins, outs, sems):
-    step = a_ref.shape[0] // cuts
-
-    def move(i, source, target, sem, part):
-        at = pl.ds(part * step, step)
-        return pltpu.make_async_copy(source.at[at], target.at[at], sem.at[i, part])
-
-    load = pltpu.make_async_copy(r_ref, res, sems.at[0])
-    load.start()
-    pieces = [(0, a_ref, a, att_ref), (1, b_ref, b, qg_ref)]
-    for part in range(cuts):
-        for i, source, buf, _ in pieces:
-            move(i, source, buf, ins, part).start()
-    load.wait()
+
+
+def finish(a_ref, b_ref, res, att_ref, qg_ref, down_ref, up_ref, down, up, sems):
+    stores = [
+        pltpu.make_async_copy(source, target, sems.at[i])
+        for i, (source, target) in enumerate(
+            [(a_ref, att_ref), (b_ref, qg_ref), (down, down_ref), (up, up_ref)]
+        )
+    ]
+    for c in stores[:2]:
+        c.start()
     reps, chunks, rank, chunk = res.shape
     half = down.shape[1] // reps
     up_half = up.shape[1] // reps
@@ -673,19 +657,8 @@
                 first, last = max(lo, half), min(hi, half + up_half)
                 base = r * up_half - half
                 up[:, base + first:base + last] = res[r, j, :, first - lo:last - lo].astype(F32)
-    stores = [
-        pltpu.make_async_copy(down, down_ref, sems.at[1]),
-        pltpu.make_async_copy(up, up_ref, sems.at[2]),
-    ]
-    for c in stores:
+    for c in stores[2:]:
         c.start()
-    for part in range(cuts):
-        for i, source, buf, target in pieces:
-            move(i, source, buf, ins, part).wait()
-            move(i, buf, target, outs, part).start()
-    for part in range(cuts):
-        for i, source, buf, target in pieces:
-            move(i, buf, target, outs, part).wait()
     for c in stores:
         c.wait()
 
@@ -712,12 +685,8 @@
     attended, query_grad, result = pl.pallas_call(
         functools.partial(kernel, slots, reps, factor),
         in_specs=[smem, smem, anywhere, anywhere, anywhere, anywhere, anywhere, vmem, anywhere],
-        out_specs=[anywhere, anywhere, vmem],
-        out_shape=[
-            jax.ShapeDtypeStruct(q.shape, BF16),
-            jax.ShapeDtypeStruct(q.shape, BF16),
-            jax.ShapeDtypeStruct((reps, chunks, rank, chunk), BF16),
-        ],
+        out_specs=[vmem, vmem, vmem],
+        out_shape=[v(q.shape, BF16), v(q.shape, BF16), v((reps, chunks, rank, chunk), BF16)],
         scratch_shapes=[
             v(x.shape, BF16), v((reps, block, width // reps), BF16), v((rank, width), BF16),
             v((heads, block, HEAD_SIZE), BF16), v((heads, block, HEAD_SIZE), BF16),
@@ -732,12 +701,11 @@
             v((KEY_HEADS, HEAD_SIZE, rows), BF16),
             v((KEY_HEADS, pairs, 2 * block, HEAD_SIZE), BF16),
             v((2 * block, 2 * rank), F32), v((KEY_HEADS, 8, rows), F32),
-            v((heads, block, HEAD_SIZE), BF16), v((heads, block, HEAD_SIZE), BF16),
             v((slots, rank, block), BF16), v((2, rank, block), F32), v((slots, rank, block), BF16),
             v((reps, rank, block), BF16),
             v((KEY_HEADS, rank, HEAD_SIZE), F32), v((reps, share, rank, HEAD_SIZE), F32),
             v((chunks, rank, chunk), BF16), v((slots, rank, chunk), BF16),
-            dma((7,)), dma((2,)),
+            dma((7,)),
             dma((slots, KEY_HEADS)), dma((slots,)), dma((slots, KEY_HEADS)),
             dma((3,)), dma((slots // 2,)), dma((slots // 2,)), dma,
             dma((3,)), dma((slots // 2,)), dma((slots // 2,)),
@@ -749,10 +717,9 @@
         ),
         name="tree_attention",
     )(parents, lengths, x, q, k, frozen, down.T, up, g)
-    cuts = 2
     attended, query_grad, down_sum, up_sum = pl.pallas_call(
-        functools.partial(finish, cuts),
-        in_specs=[anywhere, anywhere, anywhere],
+        finish,
+        in_specs=[vmem, vmem, vmem],
         out_specs=[anywhere, anywhere, anywhere, anywhere],
         out_shape=[
             jax.ShapeDtypeStruct(q.shape, BF16),
@@ -761,13 +728,10 @@
             jax.ShapeDtypeStruct((rank, up_width), F32),
         ],
         scratch_shapes=[
-            v(q.shape, BF16), v(q.shape, BF16), v(result.shape, BF16),
-            v((rank, width), F32), v((rank, up_width), F32),
-            dma((2, cuts)), dma((2, cuts)), dma((3,)),
+            v((rank, width), F32), v((rank, up_width), F32), dma((4,)),
         ],
-        compiler_params=pltpu.CompilerParams(vmem_limit_bytes=60 * 1024 * 1024),
         name="finish",
-    )(attended, query_grad, result)
+    )(*[pltpu.with_memory_space_constraint(a, pltpu.VMEM) for a in (attended, query_grad, result)])
     return attended[None], query_grad[None], down_sum.T, up_sum
 
 

time: 53.4 us -> 51.2 us (0.959)
  Pallas kernels: 52.5 us -> 50.4 us
    pallas_call x1, Pallas kernels: 2.72 us -> 1.31 us  [on_device(): pl.pallas_call(finish, in_specs=[vmem, vmem, vmem], out_specs=[anywhere,...]
    pallas_call x1, Pallas kernels: 49.8 us -> 49 us  [on_device(): pl.pallas_call(functools.partial(kernel, slots, reps, factor), in_specs=[...]
where the time goes in v6:
time: 51.2 us; the launch traced here: 51 us
  Pallas kernels  50.4 us (98%)
  between operations  0.64 us (1%)
    pallas_call x1, Pallas kernels, on_device(): pl.pallas_call(functools.partial(kernel, slots, reps, factor), in_specs=[...  49 us
    pallas_call x1, Pallas kernels, on_device(): pl.pallas_call(finish, in_specs=[vmem, vmem, vmem], out_specs=[anywhere,...  1.31 us

profile of v6, /device:TPU:0, one launch (start us, length us, event | category | flops | bytes accessed | tf_op | source)
XLA Modules:
  0.0 51.0 jit_solution(17807205494988498900)
XLA Ops:
  0.6 49.0 %tree_attention.1 = (bf16[128,2560]{1,0:T(8,128)(2,1)S(1)}, bf16[128,2560]{1,0:T(8,128)(2,1)S(1)}, bf16[2,8,32,384]{3,2,1,0:T(8,128)(2,1)S(1)}) custom-call(s32[1,8]{1,0:T(1,128)} %parents.1, s32[1,8]{1,0:T(1,128)} %lengths.1, bf16[128,5120]{1,0:T(8,128)(2,1)} %bitcast.9, bf16[128,2560]{1,0:T(8,128)(2,1)} %bitcast.10, bf16[128,512]{1,0:T(8,128)(2,1)} %bitcast.13, ...), custom_call_target="tpu_custom_call" | custom-call | tf_op jit(solution)/shard_map/tree_attention/pallas_call | solution.py:685
  49.7 1.3 %finish.1 = (bf16[128,2560]{1,0:T(8,128)(2,1)}, bf16[128,2560]{1,0:T(8,128)(2,1)}, f32[32,5120]{1,0:T(8,128)}, f32[32,512]{1,0:T(8,128)}) custom-call(bf16[128,2560]{1,0:T(8,128)(2,1)S(1)} %get-tuple-element.11.a_ref, bf16[128,2560]{1,0:T(8,128)(2,1)S(1)} %get-tuple-element.12.b_ref, bf16[2,8,32,384]{3,2,1,0:T(8,128)(2,1)S(1)} %get-tuple-element.13.res), custom_call_target="tpu_custom_call" | custom-call | tf_op jit(solution)/shard_map/finish/pallas_call | solution.py:720

commit v7 on v6

--- a/solution.py
+++ b/solution.py
@@ -53,7 +53,7 @@
     parents, lengths, x_ref, q_ref, k_ref, frozen_ref, down_ref, up_ref, g_ref,
     att_ref, qg_ref, result,
     xs, xcat, downs, qs, gs, fs, kbuf, vbuf, lowbuf, score, weight, tops, facs, acc, gup, gtr,
-    vgrad, both, invs, proj, mine, landed, tbuf, upk, upland, parts, gathered,
+    lowsum, invs, proj, mine, landed, tbuf, upk, upland, parts, gathered,
     load_sem, k_recv, l_recv, v_recv, col_send, fwd_send, on_send, turn_send, l_col, l_fwd, l_on,
     x_recv, x_send, t_recv, t_send, u_recv, u_send, p_recv, p_send,
     r_recv, r_send, a_recv, a_send, b_recv, b_send,
@@ -159,7 +159,7 @@
     pl.semaphore_wait(barrier, slots * reps - 1)
 
     class Stream:
-        def __init__(self, buf, col, fwd, on, recv, turns=False):
+        def __init__(self, buf, col, fwd, on, recv, turns=KEY_HEADS):
             self.buf, self.col, self.fwd, self.on, self.recv = buf, col, fwd, on, recv
             self.turns = turns
 
@@ -186,7 +186,7 @@
                 lambda t: self.move(own, kk, self.col.at[t], own + 2 * t).start(),
             )
 
-        def passing(self, receive, onward, across):
+        def passing(self, kk, receive, onward, across):
             def body(t):
                 slot = own - 2 * t
 
@@ -198,9 +198,9 @@
                     def _():
                         onward(slot, t)
 
-                    crosses = reaches(slot, partner)
-                    if self.turns:
-                        crosses = crosses & ((t > 1) | (own > partner))
+                    crosses = reaches(slot, partner) & (
+                        (t > 1) | (own > partner) | (kk < self.turns)
+                    )
 
                     @pl.when(crosses)
                     def _():
@@ -214,13 +214,13 @@
                 action()
 
         def forward(self, kk):
-            if self.turns:
-                @pl.when(own > partner)
+            if self.turns < KEY_HEADS:
+                @pl.when((own > partner) & (kk >= self.turns))
                 def _():
                     self.arrived(partner, kk)
-
-                self.turning(lambda: self.move(partner, kk, turn_send, own + 2).start())
+                    self.turning(lambda: self.move(partner, kk, turn_send, own + 2).start())
             self.passing(
+                kk,
                 lambda slot: self.arrived(slot, kk),
                 lambda slot, t: self.move(slot, kk, self.on.at[t], own + 2).start(),
                 lambda slot, t: self.move(slot, kk, self.fwd.at[t], partner).start(),
@@ -229,13 +229,15 @@
         def from_partner(self, t, kk):
             slot = partner - 2 * t
 
-            @pl.when(reaches(slot, own) & ((t > 0) | (not self.turns)))
+            @pl.when(reaches(slot, own) & ((t > 0) | (kk < self.turns)))
             def _():
                 self.arrived(slot, kk)
 
-    keys = Stream(kbuf, col_send, fwd_send, on_send, lambda slot, kk: k_recv.at[slot, kk])
+    keys = Stream(
+        kbuf, col_send, fwd_send, on_send, lambda slot, kk: k_recv.at[slot, kk], turns=4
+    )
     values = Stream(
-        vbuf, col_send, fwd_send, on_send, lambda slot, kk: v_recv.at[slot, kk], turns=True
+        vbuf, col_send, fwd_send, on_send, lambda slot, kk: v_recv.at[slot, kk], turns=0
     )
     lows = Stream(lowbuf, l_col, l_fwd, l_on, lambda slot, kk: l_recv.at[slot])
     each(0, KEY_HEADS, keys.send)
@@ -357,18 +359,19 @@
         lax.rem(lax.broadcasted_iota(jnp.int32, (8, rows), 1), block) < own_length
     ).astype(F32)
 
-    def weigh(kk):
-        most = tops[kk, pairs - 1]
-
-        def add(step, total):
-            fall = jnp.exp2((tops[kk, step] - most) * tune)
-            total = total + facs[kk, step] * fall
+    def add(step, totals):
+        out = []
+        for kk in range(KEY_HEADS):
+            fall = jnp.exp2((tops[kk, step] - tops[kk, pairs - 1]) * tune)
+            out.append(totals[kk] + facs[kk, step] * fall)
             facs[kk, step] = fall
-            return total
-
-        invs[kk] = live / lax.fori_loop(0, pairs, add, jnp.zeros((8, rows), F32))
-
-    each(0, KEY_HEADS, weigh)
+        return tuple(out)
+
+    totals = lax.fori_loop(
+        0, pairs, add, tuple(jnp.zeros((8, rows), F32) for _ in range(KEY_HEADS))
+    )
+    for kk in range(KEY_HEADS):
+        invs[kk] = live / totals[kk]
 
     def scatter(source, target):
         return remote(
@@ -378,23 +381,14 @@
     def project(i):
         step = pairs - 1 - i
         index = pair_at(step)
-        both[...] = jnp.zeros_like(both)
-
-        def head(kk):
+        turned = jnp.zeros((2 * rank, 2 * block), F32)
+        for kk in range(KEY_HEADS):
             fac = facs[kk, step] * invs[kk]
             facs[kk, step] = fac
             side = times(gup[kk], fac)
             high = side.astype(BF16)
-            right = jnp.concatenate(
-                [times(gtr[kk].astype(F32), fac).astype(BF16), high,
-                 (side - high.astype(F32)).astype(BF16)], axis=0,
-            )
-            out = dot(weight[kk, step], right, NT)
-            vgrad[kk, step] = out[:, :HEAD_SIZE].astype(BF16)
-            both[...] += out[:, HEAD_SIZE:]
-
-        each(0, KEY_HEADS, head)
-        turned = both[...].T
+            sides = jnp.concatenate([high, (side - high.astype(F32)).astype(BF16)], axis=0)
+            turned = turned + dot(sides, weight[kk, step], NT)
         turned = turned[:rank] + turned[rank:]
         for parity in range(2):
             slot = 2 * index + parity
@@ -427,17 +421,23 @@
     values.forward(2)
     each(0, pair + 1, lambda t: lows.from_partner(t, 0))
 
-    def low_weights(kk):
-        upk[kk] = jnp.zeros(upk.shape[1:], F32)
-
-        def one(step):
-            index = pair_at(step)
-            low = jnp.concatenate([lowbuf[2 * index, 0], lowbuf[2 * index + 1, 0]], axis=1)
-            upk[kk] += dot(low, vgrad[kk, step], NN)
-
-        each(0, pairs, one)
-
-    each(0, KEY_HEADS, low_weights)
+    for kk in range(KEY_HEADS):
+        lowsum[kk] = jnp.zeros((rank, rows), F32)
+
+    def low_weights(step):
+        index = pair_at(step)
+        low = jnp.concatenate([lowbuf[2 * index, 0], lowbuf[2 * index + 1, 0]], axis=1)
+        for kk in range(KEY_HEADS):
+            lowsum[kk] += times(dot(low, weight[kk, step], NN), facs[kk, step])
+
+    each(0, pairs, low_weights)
+    for kk in range(KEY_HEADS):
+        total = lowsum[kk]
+        high = total.astype(BF16)
+        sides = jnp.concatenate([high, (total - high.astype(F32)).astype(BF16)], axis=0)
+        out = dot(sides, stacked(gs, kk), NN)
+        upk[kk] = out[:rank] + out[rank:]
+
     values.forward(3)
     share = KEY_HEADS // reps
 
@@ -587,33 +587,41 @@
 
     other_reps(lambda r: all_of(result.at[r], b_recv.at[r]).wait())
     heads_of_two = kbuf.at[pl.ds(0, 2)]
+    turned_heads = 2 * KEY_HEADS - keys.turns - values.turns
+    turn_bytes = kbuf.at[0]
 
     def crossed(t):
-        both_cross = (t > 1) | (own > partner)
-
-        @pl.when(both_cross)
+        crossing = (t > 1) | (own > partner)
+
+        @pl.when(crossing)
         def _():
             all_of(heads_of_two, fwd_send.at[t]).wait()
 
-        @pl.when(jnp.logical_not(both_cross))
-        def _():
-            all_of(kbuf.at[0], fwd_send.at[t]).wait()
+        if keys.turns + values.turns:
+            @pl.when(jnp.logical_not(crossing))
+            def _():
+                all_of(kbuf.at[0, pl.ds(0, keys.turns + values.turns)], fwd_send.at[t]).wait()
 
     keys.targets(
         lambda: all_of(heads_of_two, fwd_send.at[0]).wait(),
         lambda t: all_of(heads_of_two, col_send.at[t]).wait(),
     )
     keys.passing(
+        0,
         lambda slot: None,
         lambda slot, t: all_of(heads_of_two, on_send.at[t]).wait(),
         lambda slot, t: crossed(t),
     )
-    values.turning(lambda: all_of(kbuf.at[0], turn_send).wait())
+    if turned_heads:
+        values.turning(
+            lambda: all_of(turn_bytes, turn_send).wait()
+        )
     lows.targets(
         lambda: all_of(lowbuf.at[0], l_fwd.at[0]).wait(),
         lambda t: all_of(lowbuf.at[0], l_col.at[t]).wait(),
     )
     lows.passing(
+        0,
         lambda slot: None,
         lambda slot, t: all_of(lowbuf.at[0], l_on.at[t]).wait(),
         lambda slot, t: all_of(lowbuf.at[0], l_fwd.at[t]).wait(),
@@ -699,8 +707,7 @@
             v((KEY_HEADS, pairs, 8, rows), F32), v((KEY_HEADS, pairs, 8, rows), F32),
             v((HEAD_SIZE, rows), F32), v((KEY_HEADS, rank, rows), F32),
             v((KEY_HEADS, HEAD_SIZE, rows), BF16),
-            v((KEY_HEADS, pairs, 2 * block, HEAD_SIZE), BF16),
-            v((2 * block, 2 * rank), F32), v((KEY_HEADS, 8, rows), F32),
+            v((KEY_HEADS, rank, rows), F32), v((KEY_HEADS, 8, rows), F32),
             v((slots, rank, block), BF16), v((2, rank, block), F32), v((slots, rank, block), BF16),
             v((reps, rank, block), BF16),
             v((KEY_HEADS, rank, HEAD_SIZE), F32), v((reps, share, rank, HEAD_SIZE), F32),

time: 51.2 us -> 48.9 us (0.955)
  Pallas kernels: 50.4 us -> 48.1 us
    pallas_call x1, Pallas kernels: 49 us -> 46.8 us  [on_device(): pl.pallas_call(functools.partial(kernel, slots, reps, factor), in_specs=[...]
where the time goes in v7:
time: 48.9 us; the launch traced here: 48.7 us
  Pallas kernels  48.1 us (98%)
  between operations  0.64 us (1%)
    pallas_call x1, Pallas kernels, on_device(): pl.pallas_call(functools.partial(kernel, slots, reps, factor), in_specs=[...  46.8 us
    pallas_call x1, Pallas kernels, on_device(): pl.pallas_call(finish, in_specs=[vmem, vmem, vmem], out_specs=[anywhere,...  1.31 us

profile of v7, /device:TPU:0, one launch (start us, length us, event | category | flops | bytes accessed | tf_op | source)
XLA Modules:
  0.0 48.7 jit_solution(2502828149867434004)
XLA Ops:
  0.6 46.8 %tree_attention.1 = (bf16[128,2560]{1,0:T(8,128)(2,1)S(1)}, bf16[128,2560]{1,0:T(8,128)(2,1)S(1)}, bf16[2,8,32,384]{3,2,1,0:T(8,128)(2,1)S(1)}) custom-call(s32[1,8]{1,0:T(1,128)} %parents.1, s32[1,8]{1,0:T(1,128)} %lengths.1, bf16[128,5120]{1,0:T(8,128)(2,1)} %bitcast.9, bf16[128,2560]{1,0:T(8,128)(2,1)} %bitcast.10, bf16[128,512]{1,0:T(8,128)(2,1)} %bitcast.13, ...), custom_call_target="tpu_custom_call" | custom-call | tf_op jit(solution)/shard_map/tree_attention/pallas_call | solution.py:693
  47.4 1.3 %finish.1 = (bf16[128,2560]{1,0:T(8,128)(2,1)}, bf16[128,2560]{1,0:T(8,128)(2,1)}, f32[32,5120]{1,0:T(8,128)}, f32[32,512]{1,0:T(8,128)}) custom-call(bf16[128,2560]{1,0:T(8,128)(2,1)S(1)} %get-tuple-element.11.a_ref, bf16[128,2560]{1,0:T(8,128)(2,1)S(1)} %get-tuple-element.12.b_ref, bf16[2,8,32,384]{3,2,1,0:T(8,128)(2,1)S(1)} %get-tuple-element.13.res), custom_call_target="tpu_custom_call" | custom-call | tf_op jit(solution)/shard_map/finish/pallas_call | solution.py:727

commit v8 on v7

--- a/solution.py
+++ b/solution.py
@@ -53,9 +53,9 @@
     parents, lengths, x_ref, q_ref, k_ref, frozen_ref, down_ref, up_ref, g_ref,
     att_ref, qg_ref, result,
     xs, xcat, downs, qs, gs, fs, kbuf, vbuf, lowbuf, score, weight, tops, facs, acc, gup, gtr,
-    lowsum, invs, proj, mine, landed, tbuf, upk, upland, parts, gathered,
+    lowsum, invs, proj, mine, landed, sums, upk, upland, parts, gathered,
     load_sem, k_recv, l_recv, v_recv, col_send, fwd_send, on_send, turn_send, l_col, l_fwd, l_on,
-    x_recv, x_send, t_recv, t_send, u_recv, u_send, p_recv, p_send,
+    x_recv, x_send, u_recv, u_send, p_recv, p_send,
     r_recv, r_send, a_recv, a_send, b_recv, b_send,
 ):
     own, rep = lax.axis_index("node"), lax.axis_index("rep")
@@ -263,6 +263,7 @@
     for kk in range(KEY_HEADS):
         vbuf[own, kk] = own_values[:, kk * HEAD_SIZE:(kk + 1) * HEAD_SIZE]
     lows.send(0)
+    each(0, KEY_HEADS, values.send)
 
     all_of(qs, load_sem.at[5]).wait()
     all_of(gs, load_sem.at[6]).wait()
@@ -347,10 +348,6 @@
 
         own_pair(kk)
 
-        @pl.when(kk == 0)
-        def _():
-            each(0, KEY_HEADS, values.send)
-
         other_pairs(kk)
 
     each(0, KEY_HEADS, arrive)
@@ -373,9 +370,10 @@
     for kk in range(KEY_HEADS):
         invs[kk] = live / totals[kk]
 
-    def scatter(source, target):
+    def scatter(source, target, r):
         return remote(
-            proj.at[target], landed.at[source], p_send.at[target], p_recv.at[source], target
+            proj.at[target], landed.at[rep, source], p_send.at[target], p_recv.at[rep, source],
+            target, r,
         )
 
     def project(i):
@@ -397,9 +395,17 @@
 
             @pl.when(reaches(slot, own))
             def _():
-                scatter(own, slot).start()
+                scatter(own, slot, rep).start()
+                other_reps(lambda r: scatter(own, slot, r).start())
+
+            @pl.when(slot == own)
+            def _():
+                other_reps(lambda r: scatter(own, own, r).start())
 
     each(0, pairs, project)
+    values.forward(1)
+    values.forward(2)
+    values.forward(3)
 
     def ancestors(action):
         def body(t):
@@ -409,16 +415,6 @@
 
         each(0, slots, body)
 
-    def descendants(action):
-        def body(t):
-            @pl.when(reaches(own, t))
-            def _():
-                action(t)
-
-        each(0, slots, body)
-
-    values.forward(1)
-    values.forward(2)
     each(0, pair + 1, lambda t: lows.from_partner(t, 0))
 
     for kk in range(KEY_HEADS):
@@ -438,7 +434,6 @@
         out = dot(sides, stacked(gs, kk), NN)
         upk[kk] = out[:rank] + out[rank:]
 
-    values.forward(3)
     share = KEY_HEADS // reps
 
     def swap_up(r):
@@ -448,38 +443,33 @@
 
     other_reps(lambda r: swap_up(r).start())
 
-    descendants(lambda t: remote(
-        proj.at[t], landed.at[t], p_send.at[t], p_recv.at[t], t
-    ).wait_recv())
-    total = mine[lax.rem(own, 2)]
-
-    def add_landed(t):
-        @pl.when(reaches(own, t))
-        def _():
-            mine[0] += landed[t].astype(F32)
-
-    mine[0] = total
-    each(0, slots, add_landed)
-    tbuf[rep] = mine[0].astype(BF16)
-
-    def swap_total(r):
-        return remote(tbuf.at[rep], tbuf.at[rep], t_send.at[r], t_recv.at[rep], own, r)
-
-    other_reps(lambda r: swap_total(r).start())
+    def land(r):
+        sums[r] = jnp.where(r == rep, mine[lax.rem(own, 2)], 0.0)
+
+        def body(t):
+            @pl.when(reaches(own, t) | (t == own) & (r != rep))
+            def _():
+                remote(
+                    proj.at[t], landed.at[r, t], p_send.at[t], p_recv.at[r, t], t, r
+                ).wait_recv()
+                sums[r] += landed[r, t].astype(F32)
+
+        each(own, slots, body)
+
+    each(0, reps, land)
     loads[3].wait()
 
     def arrivals(r):
         remote(
             x_ref.at[:, pl.ds(0, half)], xcat.at[r], x_send.at[r], x_recv.at[r], own, r
         ).wait_recv()
-        remote(tbuf.at[r], tbuf.at[r], t_send.at[r], t_recv.at[r], own, r).wait_recv()
         remote(
             upk.at[pl.ds(0, share)], upland.at[r], u_send.at[r], u_recv.at[r], own, r
         ).wait_recv()
 
     other_reps(arrivals)
 
-    projected = jnp.concatenate([tbuf[r] for r in range(reps)], axis=1)
+    projected = jnp.concatenate([sums[r] for r in range(reps)], axis=1).astype(BF16)
     ups = upk[pl.ds(rep * share, share)]
     for step in range(1, reps):
         ups = ups + upland[lax.rem(rep + step, reps)]
@@ -568,9 +558,7 @@
     def _():
         gathered[own] = parts[own]
         all_of(gathered.at[pl.ds(0, slots - 1)], r_recv).wait()
-        acc = lax.fori_loop(
-            0, slots, lambda t, a: a + gathered[t].astype(F32), jnp.zeros((rank, chunk), F32)
-        )
+        acc = jnp.sum(gathered[...].astype(F32), axis=0)
         result[rep, own] = (acc * factor).astype(BF16)
         others(lambda node: gather_copy(node, own).start())
         other_reps(lambda r: swap_result(r, own).start())
@@ -627,9 +615,9 @@
         lambda slot, t: all_of(lowbuf.at[0], l_fwd.at[t]).wait(),
     )
     other_reps(lambda r: swap_x(r).wait_send())
-    ancestors(lambda t: scatter(own, t).wait_send())
+    ancestors(lambda t: all_of(proj.at[pl.ds(0, reps)], p_send.at[t]).wait())
+    all_of(proj.at[pl.ds(0, reps - 1)], p_send.at[own]).wait()
     other_reps(lambda r: swap_up(r).wait_send())
-    other_reps(lambda r: swap_total(r).wait_send())
 
     @pl.when(own < chunks)
     def _():
@@ -708,16 +696,16 @@
             v((HEAD_SIZE, rows), F32), v((KEY_HEADS, rank, rows), F32),
             v((KEY_HEADS, HEAD_SIZE, rows), BF16),
             v((KEY_HEADS, rank, rows), F32), v((KEY_HEADS, 8, rows), F32),
-            v((slots, rank, block), BF16), v((2, rank, block), F32), v((slots, rank, block), BF16),
-            v((reps, rank, block), BF16),
+            v((slots, rank, block), BF16), v((2, rank, block), F32),
+            v((reps, slots, rank, block), BF16), v((reps, rank, block), F32),
             v((KEY_HEADS, rank, HEAD_SIZE), F32), v((reps, share, rank, HEAD_SIZE), F32),
             v((chunks, rank, chunk), BF16), v((slots, rank, chunk), BF16),
             dma((7,)),
             dma((slots, KEY_HEADS)), dma((slots,)), dma((slots, KEY_HEADS)),
             dma((3,)), dma((slots // 2,)), dma((slots // 2,)), dma,
             dma((3,)), dma((slots // 2,)), dma((slots // 2,)),
-            dma((reps,)), dma((reps,)), dma((reps,)), dma((reps,)), dma((reps,)), dma((reps,)),
-            dma((slots,)), dma((slots,)), dma, dma, dma((slots,)), dma, dma((reps,)), dma((reps,)),
+            dma((reps,)), dma((reps,)), dma((reps,)), dma((reps,)),
+            dma((reps, slots)), dma((slots,)), dma, dma, dma((slots,)), dma, dma((reps,)), dma((reps,)),
         ],
         compiler_params=pltpu.CompilerParams(
             collective_id=0, has_side_effects=True, vmem_limit_bytes=60 * 1024 * 1024

time: 48.9 us -> 48.8 us (level)
  no operation moved by 1% of the time
where the time goes in v8:
time: 48.8 us; the launch traced here: 48.6 us
  Pallas kernels  48 us (98%)
  between operations  0.64 us (1%)
    pallas_call x1, Pallas kernels, on_device(): pl.pallas_call(functools.partial(kernel, slots, reps, factor), in_specs=[...  46.7 us
    pallas_call x1, Pallas kernels, on_device(): pl.pallas_call(finish, in_specs=[vmem, vmem, vmem], out_specs=[anywhere,...  1.31 us

profile of v8, /device:TPU:0, one launch (start us, length us, event | category | flops | bytes accessed | tf_op | source)
XLA Modules:
  0.0 48.6 jit_solution(5422452599481090981)
XLA Ops:
  0.6 46.7 %tree_attention.1 = (bf16[128,2560]{1,0:T(8,128)(2,1)S(1)}, bf16[128,2560]{1,0:T(8,128)(2,1)S(1)}, bf16[2,8,32,384]{3,2,1,0:T(8,128)(2,1)S(1)}) custom-call(s32[1,8]{1,0:T(1,128)} %parents.1, s32[1,8]{1,0:T(1,128)} %lengths.1, bf16[128,5120]{1,0:T(8,128)(2,1)} %bitcast.9, bf16[128,2560]{1,0:T(8,128)(2,1)} %bitcast.10, bf16[128,512]{1,0:T(8,128)(2,1)} %bitcast.13, ...), custom_call_target="tpu_custom_call" | custom-call | tf_op jit(solution)/shard_map/tree_attention/pallas_call | solution.py:681
  47.3 1.3 %finish.1 = (bf16[128,2560]{1,0:T(8,128)(2,1)}, bf16[128,2560]{1,0:T(8,128)(2,1)}, f32[32,5120]{1,0:T(8,128)}, f32[32,512]{1,0:T(8,128)}) custom-call(bf16[128,2560]{1,0:T(8,128)(2,1)S(1)} %get-tuple-element.11.a_ref, bf16[128,2560]{1,0:T(8,128)(2,1)S(1)} %get-tuple-element.12.b_ref, bf16[2,8,32,384]{3,2,1,0:T(8,128)(2,1)S(1)} %get-tuple-element.13.res), custom_call_target="tpu_custom_call" | custom-call | tf_op jit(solution)/shard_map/finish/pallas_call | solution.py:715

commit v9 on v8

--- a/solution.py
+++ b/solution.py
@@ -175,7 +175,7 @@
             def _():
                 across()
 
-            for t in (2, 1):
+            for t in (1, 2):
                 @pl.when((own + 2 * t < slots) & reaches(own, 2 * (pair + t)))
                 def _():
                     column(t)

time: 48.8 us -> 48.1 us (0.986)
  Pallas kernels: 48 us -> 47.3 us
    pallas_call x1, Pallas kernels: 46.7 us -> 46 us  [on_device(): pl.pallas_call(functools.partial(kernel, slots, reps, factor), in_specs=[...]
where the time goes in v9:
time: 48.1 us; the launch traced here: 47.9 us
  Pallas kernels  47.3 us (98%)
  between operations  0.64 us (1%)
    pallas_call x1, Pallas kernels, on_device(): pl.pallas_call(functools.partial(kernel, slots, reps, factor), in_specs=[...  46 us
    pallas_call x1, Pallas kernels, on_device(): pl.pallas_call(finish, in_specs=[vmem, vmem, vmem], out_specs=[anywhere,...  1.31 us

profile of v9, /device:TPU:0, one launch (start us, length us, event | category | flops | bytes accessed | tf_op | source)
XLA Modules:
  0.0 47.9 jit_solution(18182797885892680158)
XLA Ops:
  0.6 46.0 %tree_attention.1 = (bf16[128,2560]{1,0:T(8,128)(2,1)S(1)}, bf16[128,2560]{1,0:T(8,128)(2,1)S(1)}, bf16[2,8,32,384]{3,2,1,0:T(8,128)(2,1)S(1)}) custom-call(s32[1,8]{1,0:T(1,128)} %parents.1, s32[1,8]{1,0:T(1,128)} %lengths.1, bf16[128,5120]{1,0:T(8,128)(2,1)} %bitcast.9, bf16[128,2560]{1,0:T(8,128)(2,1)} %bitcast.10, bf16[128,512]{1,0:T(8,128)(2,1)} %bitcast.13, ...), custom_call_target="tpu_custom_call" | custom-call | tf_op jit(solution)/shard_map/tree_attention/pallas_call | solution.py:681
  46.6 1.3 %finish.1 = (bf16[128,2560]{1,0:T(8,128)(2,1)}, bf16[128,2560]{1,0:T(8,128)(2,1)}, f32[32,5120]{1,0:T(8,128)}, f32[32,512]{1,0:T(8,128)}) custom-call(bf16[128,2560]{1,0:T(8,128)(2,1)S(1)} %get-tuple-element.11.a_ref, bf16[128,2560]{1,0:T(8,128)(2,1)S(1)} %get-tuple-element.12.b_ref, bf16[2,8,32,384]{3,2,1,0:T(8,128)(2,1)S(1)} %get-tuple-element.13.res), custom_call_target="tpu_custom_call" | custom-call | tf_op jit(solution)/shard_map/finish/pallas_call | solution.py:715

commit v10 on v9

--- a/solution.py
+++ b/solution.py
@@ -496,7 +496,11 @@
         )
 
     def others(action):
-        each(1, slots, lambda t: action(lax.rem(own + t, slots)))
+        if slots <= 8:
+            for t in range(1, slots):
+                action(lax.rem(own + t, slots))
+        else:
+            each(1, slots, lambda t: action(lax.rem(own + t, slots)))
 
     def owners(action):
         def body(node):

time: 48.1 us -> 48.1 us (level)
  no operation moved by 1% of the time
where the time goes in v10:
time: 48.1 us; the launch traced here: 47.9 us
  Pallas kernels  47.3 us (98%)
  between operations  0.64 us (1%)
    pallas_call x1, Pallas kernels, on_device(): pl.pallas_call(functools.partial(kernel, slots, reps, factor), in_specs=[...  45.9 us
    pallas_call x1, Pallas kernels, on_device(): pl.pallas_call(finish, in_specs=[vmem, vmem, vmem], out_specs=[anywhere,...  1.31 us

profile of v10, /device:TPU:0, one launch (start us, length us, event | category | flops | bytes accessed | tf_op | source)
XLA Modules:
  0.0 47.9 jit_solution(14414427913668430704)
XLA Ops:
  0.6 45.9 %tree_attention.1 = (bf16[128,2560]{1,0:T(8,128)(2,1)S(1)}, bf16[128,2560]{1,0:T(8,128)(2,1)S(1)}, bf16[2,8,32,384]{3,2,1,0:T(8,128)(2,1)S(1)}) custom-call(s32[1,8]{1,0:T(1,128)} %parents.1, s32[1,8]{1,0:T(1,128)} %lengths.1, bf16[128,5120]{1,0:T(8,128)(2,1)} %bitcast.9, bf16[128,2560]{1,0:T(8,128)(2,1)} %bitcast.10, bf16[128,512]{1,0:T(8,128)(2,1)} %bitcast.13, ...), custom_call_target="tpu_custom_call" | custom-call | tf_op jit(solution)/shard_map/tree_attention/pallas_call | solution.py:685
  46.6 1.3 %finish.1 = (bf16[128,2560]{1,0:T(8,128)(2,1)}, bf16[128,2560]{1,0:T(8,128)(2,1)}, f32[32,5120]{1,0:T(8,128)}, f32[32,512]{1,0:T(8,128)}) custom-call(bf16[128,2560]{1,0:T(8,128)(2,1)S(1)} %get-tuple-element.11.a_ref, bf16[128,2560]{1,0:T(8,128)(2,1)S(1)} %get-tuple-element.12.b_ref, bf16[2,8,32,384]{3,2,1,0:T(8,128)(2,1)S(1)} %get-tuple-element.13.res), custom_call_target="tpu_custom_call" | custom-call | tf_op jit(solution)/shard_map/finish/pallas_call | solution.py:719
